TPU v7x, 256 devices: a whole 4x4x8 slice. The times are simulated.
256 devices in a mesh: row: 16 (over y, z_lo, core), col: 16 (over x, z_hi).
Axes of the slice: x: 4, y: 4, z: 8 (z_hi: 4, z_lo: 2; z = z_hi * 2 + z_lo), core: 2. Of those that a mesh axis runs over, the one named last changes fastest.
Arguments:
- features: bfloat16 [16, 4096, 128], P('col', 'row'), may hold values from -6 to 6
- block_values: bfloat16 [16, 16, 320, 128, 128], P('row', 'col'), may hold values from -0.078125 to 0.078125
- block_row: int32 [16, 16, 320], P('row', 'col'), may hold values from 0 to 31
- block_col: int32 [16, 16, 320], P('row', 'col'), may hold values from 0 to 31
- block_occupancy: int32 [16, 16], P('row', 'col'), may hold values from 40 to 320, as said below
- weight: bfloat16 [128, 128], replicated, may hold values from -0.5 to 0.5
- cotangent: bfloat16 [16, 4096, 128], P('row', 'col'), may hold values from -6 to 6
Outputs:
- out_features: bfloat16 [16, 4096, 128], P('row', 'col')
- weight_grad: float32 [128, 128], replicated
- feature_grad: bfloat16 [16, 4096, 128], P('col', 'row')
Inputs may be any that keep to these rules, and one draw needn't show every extreme that they name: `block_occupancy`: live slots of one tile name distinct blocks; some tile has all 320 slots live in every draw.
All inputs are finite; a program needn't handle non-finite values.
Results may differ from a plain program's by a relative error of at most 0.005.
Values may be sent and summed in bfloat16 or wider, within the bound.
A program may use at most 192 MiB of HBM per device.

v0:
```python
import math

import jax
import jax.numpy as jnp
from jax import lax
from jax.sharding import PartitionSpec as P


def in_order(blocks, dim):
    dims = list(blocks.shape[1:])
    dims[dim] *= blocks.shape[0]
    return jnp.moveaxis(blocks, 0, dim).reshape(dims)


def from_everyone(array, axis):
    length = lax.axis_size(axis)
    return lax.all_to_all(
        jnp.broadcast_to(array[None], (length, *array.shape)), axis, 0, 0, tiled=True
    )


def gathered_copies(array, axis, dim):
    return in_order(from_everyone(array, axis), dim)


def split_up(array, dim, length):
    before, after = (array.shape[:dim], array.shape[dim + 1 :])
    return jnp.moveaxis(array.reshape(*before, length, -1, *after), dim, 0)


def summed_on_arrival(array, axis, dim):
    blocks = split_up(array, dim, lax.axis_size(axis))
    arrived = lax.all_to_all(blocks, axis, split_axis=0, concat_axis=0, tiled=True)
    return arrived.sum(axis=0)


def local(features, block_values, block_row, block_col, block_occupancy, weight, cotangent):
    sub_rows = features.shape[1]
    feature_width = features.shape[2]
    block_size = block_values.shape[3]
    slot_count = block_values.shape[2]
    values = block_values[0, 0]
    owned_rows_lookup = block_row[0, 0]
    cols_of = block_col[0, 0]
    live_slots = lax.iota(jnp.int32, slot_count) < block_occupancy[0, 0]
    cot_own = cotangent[0]
    column_rows = gathered_copies(features, "row", 1)[0]
    col_blocks = column_rows.shape[0] // block_size
    row_block_indices = lax.axis_size("col") * sub_rows // block_size
    picked = column_rows.reshape(col_blocks, block_size, feature_width)[cols_of]
    tile_multiplied = jnp.einsum("sab,sbf->saf", values, picked, preferred_element_type=jnp.float32)
    row_target = jnp.where(live_slots, owned_rows_lookup, row_block_indices)
    partial_output = (
        jnp.zeros((row_block_indices, block_size, feature_width), jnp.float32)
        .at[row_target]
        .add(tile_multiplied, mode="drop")
    )
    partial_output = partial_output.reshape(row_block_indices * block_size, feature_width)
    own_rows = lax.psum_scatter(partial_output, "col", scatter_dimension=0, tiled=True)
    neighbor_total = own_rows.astype(jnp.bfloat16)
    out_rows = jnp.dot(neighbor_total, weight, preferred_element_type=jnp.float32).astype(
        jnp.bfloat16
    )
    local_grad = lax.dot_general(
        neighbor_total, cot_own, (((0,), (0,)), ((), ())), preferred_element_type=jnp.float32
    )
    node_total = lax.axis_size("row") * lax.axis_size("col") * sub_rows
    weight_grad = lax.psum(local_grad, ("row", "col")) * (1.0 / math.sqrt(node_total))
    grad_own = jnp.dot(cot_own, weight.T, preferred_element_type=jnp.float32).astype(jnp.bfloat16)
    grad_rows = lax.all_gather(grad_own, "col", axis=0, tiled=True)
    grad_picked = grad_rows.reshape(row_block_indices, block_size, feature_width)[owned_rows_lookup]
    grad_products = jnp.einsum(
        "sab,saf->sbf", values, grad_picked, preferred_element_type=jnp.float32
    )
    col_target = jnp.where(live_slots, cols_of, col_blocks)
    grad_partial = (
        jnp.zeros((col_blocks, block_size, feature_width), jnp.float32)
        .at[col_target]
        .add(grad_products, mode="drop")
    )
    grad_partial = grad_partial.reshape(col_blocks * block_size, feature_width)
    feature_grad = summed_on_arrival(grad_partial, "row", 0).astype(jnp.bfloat16)
    return (out_rows[None], weight_grad, feature_grad[None])


def solution(mesh):
    in_specs = (
        P("col", "row", None),
        P("row", "col", None, None, None),
        P("row", "col", None),
        P("row", "col", None),
        P("row", "col"),
        P(),
        P("row", "col", None),
    )
    out_specs = (P("row", "col", None), P(), P("col", "row", None))
    return jax.shard_map(local, mesh=mesh, in_specs=in_specs, out_specs=out_specs, check_vma=False)
```

profile of v0, /device:TPU:1, one launch (start us, length us, event | category | flops | bytes accessed | tf_op | source)
XLA Modules:
  0.0 496.9 jit_solution(4788051507981403448)
XLA Ops:
  7.2 0.0 copy-start
  7.2 2.1 broadcast_in_dim.23
  9.2 7.3 %all-to-all-start = ((bf16[16,1,256,128]{3,2,1,0:T(8,128)(2,1)}), bf16[16,1,256,128]{3,2,1,0:T(8,128)(2,1)S(1)}, u32[]{:S(2)}, u32[]{:S(2)}) async-start(bf16[16,1,256,128]{3,2,1,0:T(8,128)(2,1)} %broadcast_in_dim.23), calls=%async_computation | async-start | bytes 2097152 | tf_op jit(solution)/shard_map/all_to_all | solution.py:17
  16.6 0.0 all-gather.2.cloned.1.call-start
  16.6 0.0 copy-done
  16.6 1.6 convolution_convert_fusion
  18.2 0.0 all-gather.2.cloned.1.call-update
  18.2 0.0 reduce-scatter.2.cloned.1.call-start
  18.9 0.7 fusion.18
  19.7 12.6 %all-to-all-done = bf16[16,1,256,128]{3,2,1,0:T(8,128)(2,1)S(1)} async-done(((bf16[16,1,256,128]{3,2,1,0:T(8,128)(2,1)}), bf16[16,1,256,128]{3,2,1,0:T(8,128)(2,1)S(1)}, u32[]{:S(2)}, u32[]{:S(2)}) %all-to-all-start) | async-done | bytes 1048608 | tf_op jit(solution)/shard_map/all_to_all | solution.py:17
  32.2 10.7 %gather_fusion = bf16[320,128,128]{2,1,0:T(8,128)(2,1)} fusion(bf16[32,128,128]{2,1,0:T(8,128)(2,1)S(1)} %bitcast.42, s32[1024]{0:T(1024)S(1)} %pad_clamp_fusion.1), kind=kCustom, calls=%fused_computation | custom fusion | bytes 20972800 | tf_op jit(solution)/shard_map/gather | solution.py:50
  43.0 15.5 %fusion.4 = f32[320,128,128]{1,2,0:T(8,128)} fusion(bf16[320,128,128]{2,1,0:T(8,128)(2,1)} %gather_fusion, bf16[1,1,320,128,128]{4,3,2,1,0:T(8,128)(2,1)} %param.8), kind=kOutput, calls=%fused_computation.8 | convolution fusion | flops 1342177280 | bytes 41943040 | tf_op jit(solution)/shard_map/sab,sbf->saf/dot_general | solution.py:51
  58.5 21.1 %copy.17 = f32[320,128,128]{2,1,0:T(8,128)} copy(f32[320,128,128]{1,2,0:T(8,128)} %fusion.4) | data formatting | bytes 41943040 | tf_op jit(solution)/shard_map/sab,sbf->saf/dot_general | solution.py:51
  79.6 0.2 broadcast.89.clone
  79.8 41.9 %scatter_fusion = f32[32,128,128]{2,1,0:T(8,128)S(1)} fusion(f32[32,128,128]{2,1,0:T(8,128)S(1)} %broadcast.89.clone, s32[320]{0:T(512)S(1)} %get-tuple-element.7, f32[320,128,128]{2,1,0:T(8,128)} %copy.17), kind=kCustom, calls=%fused_computation.2 | custom fusion | flops 5242880 | bytes 62915840 | tf_op jit(solution)/shard_map/scatter-add | solution.py:56
  121.7 0.0 copy-start.1
  121.7 1.3 copy-done.1
  123.1 0.0 reduce-scatter.2.cloned.1.call-update
  123.1 0.2 all-reduce.2.cloned.1.call-start
  123.3 0.0 all-gather.2.cloned.1.call-done
  123.4 12.0 %gather_fusion.1 = bf16[320,128,128]{2,1,0:T(8,128)(2,1)} fusion(bf16[32,128,128]{2,1,0:T(8,128)(2,1)} %bitcast.43, s32[1024]{0:T(1024)S(1)} %pad_clamp_fusion), kind=kCustom, calls=%fused_computation.1 | custom fusion | bytes 20972800 | tf_op jit(solution)/shard_map/gather | solution.py:71
  135.4 13.2 %fusion.7 = f32[320,128,128]{1,2,0:T(8,128)} fusion(bf16[320,128,128]{2,1,0:T(8,128)(2,1)} %gather_fusion.1, bf16[1,1,320,128,128]{4,3,2,1,0:T(8,128)(2,1)} %param.8), kind=kOutput, calls=%fused_computation.9 | convolution fusion | flops 1342177280 | bytes 41943040 | tf_op jit(solution)/shard_map/sab,saf->sbf/dot_general | solution.py:72
  148.6 21.2 %copy.19 = f32[320,128,128]{2,1,0:T(8,128)} copy(f32[320,128,128]{1,2,0:T(8,128)} %fusion.7) | data formatting | bytes 41943040 | tf_op jit(solution)/shard_map/sab,saf->sbf/dot_general | solution.py:72
  169.8 0.2 broadcast.89.clone.1
  170.0 0.0 copy-start.2
  170.0 41.9 %scatter_fusion.1 = f32[32,128,128]{2,1,0:T(8,128)S(1)} fusion(f32[32,128,128]{2,1,0:T(8,128)S(1)} %broadcast.89.clone.1, s32[320]{0:T(512)S(1)} %get-tuple-element.5, f32[320,128,128]{2,1,0:T(8,128)} %copy.19), kind=kCustom, calls=%fused_computation.3 | custom fusion | flops 5242880 | bytes 62915840 | tf_op jit(solution)/shard_map/scatter-add | solution.py:79
  211.9 30.6 %all_to_all.10 = f32[16,256,128]{2,1,0:T(8,128)} all-to-all(f32[16,256,128]{2,1,0:T(8,128)S(1)} %bitcast.41), channel_id=1, replica_groups=mesh['row'=16,'col'=16] {'row'}, dimensions={0} | all-to-all | bytes 4194304 | tf_op jit(solution)/shard_map/all_to_all | solution.py:33
  242.5 2.3 reduce_sum.9
  244.9 0.0 reduce-scatter.2.cloned.1.call-done
  244.9 1.7 fusion.12
  246.6 0.0 all-reduce.2.cloned.1.call-update
  246.6 0.0 copy-done.2
  246.6 1.7 fusion.10
  248.3 240.6 %all-reduce.2.cloned.1.call-done = f32[128,128]{1,0:T(8,128)} async-done(((f32[128,128]{1,0:T(8,128)}), f32[128,128]{1,0:T(8,128)}) %all-reduce.2.cloned.1.call-update) | async-done | bytes 65552 | tf_op jit(solution)/shard_map/psum | solution.py:68
  488.9 1.5 broadcast_multiply_fusion
  (2 shorter events, 0.0 us)
Async XLA Ops:
  7.2 9.5 %copy-start = (bf16[1,256,128]{2,1,0:T(8,128)(2,1)S(1)}, bf16[1,256,128]{2,1,0:T(8,128)(2,1)}, u32[]{:S(2)}) copy-start(bf16[1,256,128]{2,1,0:T(8,128)(2,1)} %param.13) | copy-start | bytes 196612
  9.2 23.0 %all-to-all-start = ((bf16[16,1,256,128]{3,2,1,0:T(8,128)(2,1)}), bf16[16,1,256,128]{3,2,1,0:T(8,128)(2,1)S(1)}, u32[]{:S(2)}, u32[]{:S(2)}) async-start(bf16[16,1,256,128]{3,2,1,0:T(8,128)(2,1)} %broadcast_in_dim.23), calls=%async_computation | async-start | bytes 2097152 | tf_op jit(solution)/shard_map/all_to_all | solution.py:17
  16.6 106.8 %all-gather.2.cloned.1.call-start = ((), (), s32[]{:S(2)}) async-start(), calls=%async_computation.5 | async-start | bytes 1114112 | tf_op jit(solution)/shard_map/all_gather | solution.py:70
  18.2 226.7 %reduce-scatter.2.cloned.1.call-start = ((), (), s32[]{:S(2)}) async-start(), calls=%async_computation.3 | async-start | bytes 2228224 | tf_op jit(solution)/shard_map/reduce_scatter | solution.py:59
  121.7 1.4 copy-start.1
  123.1 365.8 %all-reduce.2.cloned.1.call-start = ((), (), s32[]{:S(2)}) async-start(), calls=%async_computation.4 | async-start | bytes 131072 | tf_op jit(solution)/shard_map/psum | solution.py:68
  170.0 76.6 %copy-start.2 = (bf16[128,128]{1,0:T(8,128)(2,1)S(1)}, bf16[128,128]{1,0:T(8,128)(2,1)}, u32[]{:S(2)}) copy-start(bf16[128,128]{1,0:T(8,128)(2,1)} %param.12) | copy-start | bytes 98308
Sparse Core Ops, SparseCore 0:
  20.4 53.3 all-gather.1
  123.2 87.8 reduce-scatter.1
  246.7 242.1 all-reduce.1
where the time goes:
time: 500 us; the launch traced here: 497 us
  waiting for transfers between devices  253 us (51%)
  other arithmetic  88.4 us (18%)
  local copies, waits for them, and re-layouts  68.9 us (14%)
  matrix products  33.7 us (7%)
  blocking collectives  30.6 us (6%)
  between operations  14.5 us (3%)
  starting transfers between devices  7.63 us (2%)
    psum x1, waiting for transfers between devices, local(): lax.psum(local_grad, ('row', 'col')) * (1.0 / math.sqrt(node_total))  241 us
    scatter-add x1, other arithmetic, local(): grad_partial = jnp.zeros((col_blocks, block_size, feature_width), jnp.flo...  41.9 us
    scatter-add x1, other arithmetic, local(): partial_output = jnp.zeros((row_block_indices, block_size, feature_width)...  41.9 us
    all_to_all x1, blocking collectives, summed_on_arrival(): lax.all_to_all(blocks, axis, split_axis=0, concat_axis=0, tiled=True)  30.6 us
    dot_general x1, local copies, waits for them, and re-layouts, local(): jnp.einsum('sab,saf->sbf', values, grad_picked, preferred_element_type=jn...  21.2 us
    dot_general x1, local copies, waits for them, and re-layouts, local(): jnp.einsum('sab,sbf->saf', values, picked, preferred_element_type=jnp.flo...  21.1 us
    dot_general x1, matrix products, local(): jnp.einsum('sab,sbf->saf', values, picked, preferred_element_type=jnp.flo...  15.5 us
    dot_general x1, matrix products, local(): jnp.einsum('sab,saf->sbf', values, grad_picked, preferred_element_type=jn...  13.2 us
  transfers between devices with their start and end apart: 4, of which 2 were waited for; matrix products, arithmetic and copies ran while one was open for 37% of the time, Pallas kernels for 0%

commit v1 on v0

v1 whole, which is shorter than its diff:
```python
import functools
import math

import jax
import jax.numpy as jnp
from jax import lax
from jax.experimental import pallas as pl
from jax.experimental.pallas import tpu as pltpu
from jax.sharding import PartitionSpec as P

MESH = pl.DeviceIdType.MESH
F32 = jnp.float32
BF16 = jnp.bfloat16
VM = pl.BlockSpec(memory_space=pltpu.VMEM)
UNROLL = 8


def place():
    r, c = lax.axis_index("row"), lax.axis_index("col")
    return r // 4, (r // 2) % 2, r % 2, c // 4, c % 4


def device(where, dy=0, dl=0, dc=0, dx=0, dz=0):
    y, l, k, x, z = where
    row = ((y + dy + 4) % 4) * 4 + ((l + dl) % 2) * 2 + (k + dc) % 2
    col = ((x + dx + 4) % 4) * 4 + (z + dz + 4) % 4
    return (row, col)


def meet(peers):
    barrier = pltpu.get_barrier_semaphore()
    for peer in peers:
        pl.semaphore_signal(barrier, inc=1, device_id=peer, device_id_type=MESH)
    pl.semaphore_wait(barrier, len(peers))


class Mail:
    def __init__(self, send_sems, recv_sems):
        self.send_sems, self.recv_sems = send_sems, recv_sems
        self.copies, self.waiting = {}, {}

    def send(self, key, src, dst, peer):
        i = len(self.copies)
        copy = pltpu.make_async_remote_copy(
            src_ref=src,
            dst_ref=dst,
            send_sem=self.send_sems.at[i],
            recv_sem=self.recv_sems.at[i],
            device_id=peer,
            device_id_type=MESH,
        )
        copy.start()
        self.copies[key] = copy
        self.waiting[key] = copy

    def take(self, *keys):
        for key in keys:
            if key in self.waiting:
                self.waiting.pop(key).wait_recv()

    def finish(self):
        self.take(*list(self.waiting))
        for copy in self.copies.values():
            copy.wait_send()


GATHER_COPIES = 6 + 24 + 1 + 12 + 8


def gather_kernel(f_ref, c_ref, fall, call, send_sems, recv_sems):
    where = place()
    y, l, k, x, z = where
    dev = functools.partial(device, where)
    xp, xm, zp, zm = dev(dx=1), dev(dx=-1), dev(dz=1), dev(dz=-1)
    yp, ym, lo, other = dev(dy=1), dev(dy=-1), dev(dl=1), dev(dc=1)
    meet([xp, xm, zp, zm, yp, ym, lo, other])
    mail = Mail(send_sems, recv_sems)

    def cat(dx, dz, h):
        return call.at[(((x + dx + 4) % 4) * 4 + (z + dz + 4) % 4) * 2 + h]

    def fat(dy, dl, h):
        return fall.at[(((y + dy + 4) % 4) * 4 + ((l + dl) % 2) * 2 + k) * 2 + h]

    def fboth(dy, dl):
        return fall.at[pl.ds((((y + dy + 4) % 4) * 4 + ((l + dl) % 2) * 2 + k) * 2, 2)]

    def xsend(d, h, p):
        src = c_ref.at[h] if d == 0 else cat(0, d, h)
        mail.send(("x", d, h, p), src, cat(0, d, h), xp if p > 0 else xm)

    def zsend(h, p):
        mail.send(("z", h, p), c_ref.at[h], cat(0, 0, h), zp if p > 0 else zm)

    def ysend(e, h, p):
        src = f_ref.at[h] if e == 0 else fat(0, e, h)
        mail.send(("y", e, h, p), src, fat(0, e, h), yp if p > 0 else ym)

    def xrelay(d):
        mail.take(("x", d, 0, 1))
        mail.send(("xr", d, 1), cat(-1, d, 0), cat(-1, d, 0), xp)
        mail.take(("x", d, 1, -1))
        mail.send(("xr", d, -1), cat(1, d, 1), cat(1, d, 1), xm)

    def yrelay(e):
        mail.take(("y", e, 0, 1))
        mail.send(("yr", e, 1), fat(-1, e, 0), fat(-1, e, 0), yp)
        mail.take(("y", e, 1, -1))
        mail.send(("yr", e, -1), fat(1, e, 1), fat(1, e, 1), ym)

    def share(dy, dl):
        src = f_ref if (dy, dl) == (0, 0) else fboth(dy, dl)
        mail.send(("k", dy, dl), src, fboth(dy, dl), other)

    for h, p in ((0, 1), (1, -1), (1, 1), (0, -1)):
        zsend(h, p)
        xsend(0, h, p)
        if (h, p) == (0, 1):
            mail.send(("l",), f_ref, fboth(0, 0), lo)
        ysend(0, h, p)
    share(0, 0)
    call[pl.ds(((x * 4) + z) * 2, 2)] = c_ref[...]
    fall[pl.ds((y * 4 + l * 2 + k) * 2, 2)] = f_ref[...]

    xrelay(0)
    yrelay(0)
    mail.take(("l",))
    for h, p in ((0, 1), (1, -1), (1, 1), (0, -1)):
        ysend(1, h, p)
    mail.take(("z", 0, 1))
    mail.send(("zr", 1), cat(0, -1, 0), cat(0, -1, 0), zp)
    xsend(-1, 0, 1)
    xsend(-1, 0, -1)
    mail.take(("z", 1, -1))
    mail.send(("zr", -1), cat(0, 1, 1), cat(0, 1, 1), zm)
    xsend(1, 1, 1)
    xsend(1, 1, -1)
    mail.take(("z", 1, 1))
    xsend(-1, 1, 1)
    xsend(-1, 1, -1)
    mail.take(("z", 0, -1))
    xsend(1, 0, 1)
    xsend(1, 0, -1)
    share(0, 1)
    mail.take(("y", 0, 1, 1))
    share(-1, 0)
    mail.take(("y", 0, 0, -1))
    share(1, 0)
    yrelay(1)
    xrelay(-1)
    mail.take(("zr", 1))
    xsend(2, 0, 1)
    xsend(2, 0, -1)
    mail.take(("zr", -1))
    xsend(2, 1, 1)
    xsend(2, 1, -1)
    xrelay(1)
    mail.take(("yr", 0, 1), ("yr", 0, -1))
    share(2, 0)
    mail.take(("y", 1, 1, 1))
    share(-1, 1)
    mail.take(("y", 1, 0, -1))
    share(1, 1)
    mail.take(("yr", 1, 1), ("yr", 1, -1))
    share(2, 1)
    xrelay(2)
    mail.finish()


def gather(features, cotangent):
    blocks = jax.ShapeDtypeStruct((32, 128, 128), BF16)
    return pl.pallas_call(
        gather_kernel,
        out_shape=(blocks, blocks),
        in_specs=[VM, VM],
        out_specs=(VM, VM),
        scratch_shapes=[
            pltpu.SemaphoreType.DMA((GATHER_COPIES,)),
            pltpu.SemaphoreType.DMA((GATHER_COPIES,)),
        ],
        compiler_params=pltpu.CompilerParams(collective_id=0, has_side_effects=True),
        name="gather_both",
    )(features, cotangent)


def tile_kernel(rows, cols, live, x_ref, c_ref, w_ref, v_hbm, p_ref, q_ref, g_ref, v_buf, acc_p, acc_q, grad_t, sems):
    blocks = x_ref.shape[0]
    slots = v_hbm.shape[0]
    chunks = sems.shape[0]
    per = slots // chunks
    count = live[0]

    def fetch(i):
        part = pl.ds(i * per, per)
        return pltpu.make_async_copy(v_hbm.at[part], v_buf.at[part], sems.at[i])

    for i in range(chunks):
        pl.when(i * per < count)(lambda i=i: fetch(i).start())
    weight = w_ref[...]
    for j in range(blocks):
        grad_t[j] = lax.dot_general(
            weight, c_ref[j], (((1,), (1,)), ((), ())), preferred_element_type=F32
        ).astype(BF16)
    acc_p[...] = jnp.zeros_like(acc_p)
    acc_q[...] = jnp.zeros_like(acc_q)

    def group(g, _):
        base = g * UNROLL
        for u in range(UNROLL):
            s = base + u
            r, c = rows[s], cols[s]
            alive = s < count
            block = v_buf[s]
            fwd = jnp.dot(block, x_ref[c], preferred_element_type=F32)
            bwd = jnp.dot(grad_t[r], block, preferred_element_type=F32)
            rt = jnp.where(alive, r, blocks)
            ct = jnp.where(alive, c, blocks)
            acc_p[rt] += fwd
            acc_q[ct] += bwd
        return 0

    groups = per // UNROLL
    for i in range(chunks):
        @pl.when(i * per < count)
        def _():
            fetch(i).wait()
            left = jnp.minimum((count - i * per + UNROLL - 1) // UNROLL, groups)
            lax.fori_loop(i * groups, i * groups + left, group, 0)

    total = jnp.zeros(g_ref.shape, F32)
    for j in range(blocks):
        part = acc_p[j].astype(BF16)
        p_ref[j] = part
        q_ref[j] = acc_q[j].T.astype(BF16)
        total += lax.dot_general(
            part, c_ref[j], (((0,), (0,)), ((), ())), preferred_element_type=F32
        )
    g_ref[...] = total


def tile(rows, cols, live, xs, cs, weight, values):
    blocks = jax.ShapeDtypeStruct(xs.shape, BF16)
    n, b, f = xs.shape
    slots = values.shape[0]
    chunks = 10 if slots % (10 * UNROLL) == 0 else 1
    return pl.pallas_call(
        tile_kernel,
        out_shape=(blocks, blocks, jax.ShapeDtypeStruct((f, f), F32)),
        grid_spec=pltpu.PrefetchScalarGridSpec(
            num_scalar_prefetch=3,
            in_specs=[VM, VM, VM, pl.BlockSpec(memory_space=pl.ANY)],
            out_specs=(VM, VM, VM),
            scratch_shapes=[
                pltpu.VMEM((slots, b, b), BF16),
                pltpu.VMEM((n + 1, b, f), F32),
                pltpu.VMEM((n + 1, f, b), F32),
                pltpu.VMEM((n, f, b), BF16),
                pltpu.SemaphoreType.DMA((chunks,)),
            ],
        ),
        compiler_params=pltpu.CompilerParams(vmem_limit_bytes=40 * 1024 * 1024),
        name="tile_products",
    )(rows, cols, live, xs, cs, weight, values)


SCATTER_COPIES = 24 + 6 + 8 + 12 + 1 + (1 + 3 + 3 + 1 + 3 + 3 + 1)


def scatter_kernel(scale, p_ref, q_ref, g_ref, w_ref, out_ref, wg_ref, fg_ref,
                   xr_buf, x_buf, xs_buf, zr_buf, z_buf, zs_buf, s_buf,
                   k_buf, t_buf, yr_buf, y_buf, ys_buf, u_buf, l_buf,
                   gk_buf, gx_buf, gy_buf, gl_buf, gz_buf, gs_buf, send_sems, recv_sems):
    where = place()
    y, l, k, x, z = where
    dev = functools.partial(device, where)
    xp, xm, zp, zm = dev(dx=1), dev(dx=-1), dev(dz=1), dev(dz=-1)
    yp, ym, lo, other = dev(dy=1), dev(dy=-1), dev(dl=1), dev(dc=1)
    meet([xp, xm, zp, zm, yp, ym, lo, other, dev(dx=2), dev(dy=2), dev(dz=2)])
    mail = Mail(send_sems, recv_sems)

    def pat(dx, dz, h):
        return p_ref.at[(((x + dx + 4) % 4) * 4 + (z + dz + 4) % 4) * 2 + h]

    def chip(dy, dl):
        return ((y + dy + 4) % 4) * 2 + (l + dl) % 2

    def add(*refs):
        total = refs[0][...].astype(F32)
        for ref in refs[1:]:
            total = total + ref[...].astype(F32)
        return total

    def xrelay(d):
        i = d % 4
        mail.send(("xr", d, 1), pat(2, d, 0), xr_buf.at[i, 0], xp)
        mail.send(("xr", d, -1), pat(2, d, 1), xr_buf.at[i, 1], xm)

    def xplain(d):
        i = d % 4
        mail.send(("x", d, 1, 1), pat(1, d, 1), x_buf.at[i, 0, 1], xp)
        mail.send(("x", d, 0, -1), pat(-1, d, 0), x_buf.at[i, 1, 0], xm)

    def xsum(d):
        i = d % 4
        mail.take(("xr", d, 1))
        xs_buf[i, 0] = add(pat(1, d, 0), xr_buf.at[i, 0]).astype(BF16)
        mail.send(("x", d, 0, 1), xs_buf.at[i, 0], x_buf.at[i, 0, 0], xp)
        mail.take(("xr", d, -1))
        xs_buf[i, 1] = add(pat(-1, d, 1), xr_buf.at[i, 1]).astype(BF16)
        mail.send(("x", d, 1, -1), xs_buf.at[i, 1], x_buf.at[i, 1, 1], xm)

    def xtotal(d, h):
        i = d % 4
        mail.take(("x", d, h, 1), ("x", d, h, -1))
        return add(pat(0, d, h), x_buf.at[i, 0, h], x_buf.at[i, 1, h])

    def ksend(dy, dl):
        i = chip(dy, dl)
        mail.send(("k", dy, dl), q_ref.at[i, (k + 1) % 2], k_buf.at[i], other)

    def ktake(dy, dl):
        i = chip(dy, dl)
        mail.take(("k", dy, dl))
        t_buf[i] = add(q_ref.at[i, k], k_buf.at[i]).astype(BF16)

    def yrelay(e):
        i = chip(2, e)
        mail.send(("yr", e, 1), t_buf.at[i, 0], yr_buf.at[e, 0], yp)
        mail.send(("yr", e, -1), t_buf.at[i, 1], yr_buf.at[e, 1], ym)

    def yplain(e):
        mail.send(("y", e, 1, 1), t_buf.at[chip(1, e), 1], y_buf.at[e, 0, 1], yp)
        mail.send(("y", e, 0, -1), t_buf.at[chip(-1, e), 0], y_buf.at[e, 1, 0], ym)

    def ysum(e):
        mail.take(("yr", e, 1))
        ys_buf[e, 0] = add(t_buf.at[chip(1, e), 0], yr_buf.at[e, 0]).astype(BF16)
        mail.send(("y", e, 0, 1), ys_buf.at[e, 0], y_buf.at[e, 0, 0], yp)
        mail.take(("yr", e, -1))
        ys_buf[e, 1] = add(t_buf.at[chip(-1, e), 1], yr_buf.at[e, 1]).astype(BF16)
        mail.send(("y", e, 1, -1), ys_buf.at[e, 1], y_buf.at[e, 1, 1], ym)

    def ytotal(e, h):
        mail.take(("y", e, h, 1), ("y", e, h, -1))
        return add(t_buf.at[chip(0, e), h], y_buf.at[e, 0, h], y_buf.at[e, 1, h])

    half, piece = 64, 16
    mine = pl.multiple_of(k * half, half)
    theirs = pl.multiple_of((1 - k) * half, half)
    mail.send(("gk",), g_ref.at[pl.ds(theirs, half)], gk_buf, other)
    for d in (2, 1, -1, 0):
        xrelay(d)
    for dl in (1, 0):
        for dy in (2, 1, -1, 0):
            ksend(dy, dl)
    xplain(2)

    mail.take(("gk",))
    gs_buf[0] = g_ref[pl.ds(mine, half)] + gk_buf[...]
    for d in (1, 2, 3):
        to = (x + d) % 4
        mail.send(("gx", d), gs_buf.at[0, pl.ds(pl.multiple_of(to * piece, piece), piece)],
                  gx_buf.at[x], dev(dx=d))
    gx_buf[x] = gs_buf[0, pl.ds(pl.multiple_of(x * piece, piece), piece)]

    ktake(2, 1)
    yrelay(1)
    xsum(2)
    xplain(1)
    ktake(1, 1)
    ktake(-1, 1)
    yplain(1)
    ktake(0, 1)
    ktake(2, 0)
    yrelay(0)
    xsum(1)
    xplain(-1)
    mail.take(("gx", 1), ("gx", 2), ("gx", 3))
    gy_buf[y] = (gx_buf[0] + gx_buf[1]) + (gx_buf[2] + gx_buf[3])
    for d in (1, 2, 3):
        mail.send(("gy", d), gy_buf.at[y], gy_buf.at[y], dev(dy=d))
    ktake(1, 0)
    ktake(-1, 0)
    yplain(0)
    ktake(0, 0)
    ysum(1)
    xsum(-1)
    xplain(0)
    ysum(0)
    xsum(0)

    s_buf[2, 0] = xtotal(2, 0).astype(BF16)
    mail.send(("zr", 1), s_buf.at[2, 0], zr_buf.at[0], zp)
    s_buf[2, 1] = xtotal(2, 1).astype(BF16)
    mail.send(("zr", -1), s_buf.at[2, 1], zr_buf.at[1], zm)
    mail.take(("gy", 1), ("gy", 2), ("gy", 3))
    gl_buf[l] = (gy_buf[0] + gy_buf[1]) + (gy_buf[2] + gy_buf[3])
    mail.send(("gl",), gl_buf.at[l], gl_buf.at[l], lo)
    s_buf[1, 1] = xtotal(1, 1).astype(BF16)
    mail.send(("z", 1, 1), s_buf.at[1, 1], z_buf.at[0, 1], zp)
    s_buf[3, 0] = xtotal(-1, 0).astype(BF16)
    mail.send(("z", 0, -1), s_buf.at[3, 0], z_buf.at[1, 0], zm)
    for h in range(2):
        u_buf[h] = ytotal(1, h).astype(BF16)
    mail.send(("l",), u_buf, l_buf, lo)
    mail.take(("gl",))
    gz_buf[z] = gl_buf[0] + gl_buf[1]
    for d in (1, 2, 3):
        mail.send(("gz", d), gz_buf.at[z], gz_buf.at[z], dev(dz=d))
    total = xtotal(1, 0)
    mail.take(("zr", 1))
    zs_buf[0] = (total + zr_buf[0].astype(F32)).astype(BF16)
    mail.send(("z", 0, 1), zs_buf.at[0], z_buf.at[0, 0], zp)
    total = xtotal(-1, 1)
    mail.take(("zr", -1))
    zs_buf[1] = (total + zr_buf[1].astype(F32)).astype(BF16)
    mail.send(("z", 1, -1), zs_buf.at[1], z_buf.at[1, 1], zm)

    mail.take(("gz", 1), ("gz", 2), ("gz", 3))
    place_x = pl.ds(pl.multiple_of(k * half + x * piece, piece), piece)
    wg_sum = ((gz_buf[0] + gz_buf[1]) + (gz_buf[2] + gz_buf[3])) * scale
    gs_buf[1, pl.ds(pl.multiple_of(x * piece, piece), piece)] = wg_sum
    for d in (1, 2, 3):
        mine_x = gs_buf.at[1, pl.ds(pl.multiple_of(x * piece, piece), piece)]
        mail.send(("ga", d), mine_x, mine_x, dev(dx=d))
    mail.take(("l",))
    for h in range(2):
        fg_ref[h] = (ytotal(0, h) + l_buf[h].astype(F32)).astype(BF16)
    mail.take(("ga", 1), ("ga", 2), ("ga", 3))
    mail.send(("gb",), gs_buf.at[1], wg_ref.at[pl.ds(mine, half)], other)
    wg_ref[pl.ds(mine, half)] = gs_buf[1]

    for h in range(2):
        total = xtotal(0, h)
        mail.take(("z", h, 1), ("z", h, -1))
        agg = (total + z_buf[0, h].astype(F32) + z_buf[1, h].astype(F32)).astype(BF16)
        out_ref[h] = jnp.dot(agg, w_ref[...], preferred_element_type=F32).astype(BF16)
    mail.finish()


def scatter(ps, qs, grads, weight, scale):
    b = ps.shape[1:]
    own = jax.ShapeDtypeStruct((2, *b), BF16)
    half = lambda *lead: pltpu.VMEM((*lead, *b), BF16)
    piece = lambda n: pltpu.VMEM((n, 16, 128), F32)
    return pl.pallas_call(
        functools.partial(scatter_kernel, scale),
        out_shape=(own, jax.ShapeDtypeStruct(grads.shape, F32), own),
        in_specs=[VM] * 4,
        out_specs=(VM,) * 3,
        scratch_shapes=[
            half(4, 2), half(4, 2, 2), half(4, 2), half(2), half(2, 2), half(2), half(4, 2),
            half(8, 2), half(8, 2), half(2, 2), half(2, 2, 2), half(2, 2), half(2), half(2),
            pltpu.VMEM((64, 128), F32), piece(4), piece(4), piece(2), piece(4),
            pltpu.VMEM((2, 64, 128), F32),
            pltpu.SemaphoreType.DMA((SCATTER_COPIES,)),
            pltpu.SemaphoreType.DMA((SCATTER_COPIES,)),
        ],
        compiler_params=pltpu.CompilerParams(collective_id=1, has_side_effects=True),
        name="scatter_both",
    )(ps, qs.reshape(8, 2, 2, *b), grads, weight)


def local(features, block_values, block_row, block_col, block_occupancy, weight, cotangent):
    width = features.shape[2]
    block = block_values.shape[3]
    nodes = lax.axis_size("row") * lax.axis_size("col") * features.shape[1]
    xs, cs = gather(features.reshape(-1, block, width), cotangent.reshape(-1, block, width))
    ps, qs, grads = tile(
        block_row[0, 0], block_col[0, 0], block_occupancy[0], xs, cs, weight, block_values[0, 0]
    )
    out, wgrad, fgrad = scatter(ps, qs, grads, weight, 1.0 / math.sqrt(nodes))
    return (out.reshape(features.shape), wgrad, fgrad.reshape(features.shape))


def solution(mesh):
    in_specs = (
        P("col", "row", None),
        P("row", "col", None, None, None),
        P("row", "col", None),
        P("row", "col", None),
        P("row", "col"),
        P(),
        P("row", "col", None),
    )
    out_specs = (P("row", "col", None), P(), P("col", "row", None))
    return jax.shard_map(local, mesh=mesh, in_specs=in_specs, out_specs=out_specs, check_vma=False)
```

time: 500 us -> 83.6 us (0.17)
  waiting for transfers between devices: 253 us -> 0 us
  other arithmetic: 88.4 us -> 1.4 us
  Pallas kernels: 0 us -> 69.8 us
  local copies, waits for them, and re-layouts: 68.9 us -> 10.2 us
  matrix products: 33.7 us -> 0 us
  blocking collectives: 30.6 us -> 0 us
  between operations: 14.5 us -> 1.32 us
  starting transfers between devices: 7.63 us -> 0 us
    psum x1 -> x0, waiting for transfers between devices: 241 us -> none  [local(): lax.psum(local_grad, ('row', 'col')) * (1.0 / math.sqrt(node_total))]
    scatter-add x2 -> x0, other arithmetic: 83.8 us -> none  [the longest x1 41.9 us: local(): grad_partial = jnp.zeros((col_blocks, block_size, feature_width), jnp.flo...]
    pallas_call x0 -> x3, Pallas kernels: none -> 69.8 us  [the longest x1 37.4 us: scatter(): pl.pallas_call(functools.partial(scatter_kernel, scale), out_shape=(own,...]
    dot_general x2 -> x0, local copies, waits for them, and re-layouts: 42.3 us -> none  [the longest x1 21.2 us: local(): jnp.einsum('sab,saf->sbf', values, grad_picked, preferred_element_type=jn...]
    dot_general x5 -> x0, matrix products: 33.7 us -> none  [the longest x1 15.5 us: local(): jnp.einsum('sab,sbf->saf', values, picked, preferred_element_type=jnp.flo...]
    all_to_all x1 -> x0, blocking collectives: 30.6 us -> none  [summed_on_arrival(): lax.all_to_all(blocks, axis, split_axis=0, concat_axis=0, tiled=True)]
    gather x2 -> x0, local copies, waits for them, and re-layouts: 22.7 us -> none  [the longest x1 12 us: local(): grad_rows.reshape(row_block_indices, block_size, feature_width)]
    all_to_all x1 -> x0, waiting for transfers between devices: 12.6 us -> none  [from_everyone(): lax.all_to_all(jnp.broadcast_to(array[None], (length, *array.shape)), axi...]
  transfers between devices with their start and end apart: 4 -> 0, of which waited for: 2 -> 0; matrix products, arithmetic and copies ran while one was open for 37% -> 0% of each run, Pallas kernels for 0% -> 0%
where the time goes in v1:
time: 83.6 us; the launch traced here: 82.7 us
  Pallas kernels  69.8 us (83%)
  local copies, waits for them, and re-layouts  10.2 us (12%)
  other arithmetic  1.4 us (2%)
  between operations  1.32 us (2%)
    pallas_call x1, Pallas kernels, scatter(): pl.pallas_call(functools.partial(scatter_kernel, scale), out_shape=(own,...  37.4 us
    pallas_call x1, Pallas kernels, gather(): pl.pallas_call(gather_kernel, out_shape=(blocks, blocks), in_specs=[VM, V...  26.4 us
    unnamed x15, local copies, waits for them, and re-layouts  10.2 us
    pallas_call x1, Pallas kernels, tile(): pl.pallas_call(tile_kernel, out_shape=(blocks, blocks, jax.ShapeDtypeStru...  5.94 us

profile of v1, /device:TPU:1, one launch (start us, length us, event | category | flops | bytes accessed | tf_op | source)
XLA Modules:
  0.0 82.7 jit_solution(15336632347925119666)
XLA Ops:
  1.3 0.7 reduce.rows
  2.0 0.7 reduce.1.cols
  2.7 26.4 %gather_both.1 = (bf16[32,128,128]{2,1,0:T(8,128)(2,1)}, bf16[32,128,128]{2,1,0:T(8,128)(2,1)}) custom-call(bf16[2,128,128]{2,1,0:T(8,128)(2,1)} %bitcast.10, bf16[2,128,128]{2,1,0:T(8,128)(2,1)} %bitcast.11), custom_call_target="tpu_custom_call" | custom-call | tf_op jit(solution)/shard_map/gather_both/pallas_call | solution.py:172
  29.1 0.0 copy-start
  29.1 1.2 %copy-done = bf16[32,128,128]{2,1,0:T(8,128)(2,1)S(1)} copy-done((bf16[32,128,128]{2,1,0:T(8,128)(2,1)S(1)}, bf16[32,128,128]{2,1,0:T(8,128)(2,1)}, u32[]{:S(2)}) %copy-start) | copy-done | bytes 1048600
  30.3 0.0 copy-start.1
  30.3 1.2 %copy-done.1 = bf16[32,128,128]{2,1,0:T(8,128)(2,1)S(1)} copy-done((bf16[32,128,128]{2,1,0:T(8,128)(2,1)S(1)}, bf16[32,128,128]{2,1,0:T(8,128)(2,1)}, u32[]{:S(2)}) %copy-start.1) | copy-done | bytes 1048600
  31.6 0.0 copy-start.4
  31.6 0.8 copy-done.4
  32.3 5.9 %tile_products.1 = (bf16[32,128,128]{2,1,0:T(8,128)(2,1)S(1)}, bf16[32,128,128]{2,1,0:T(8,128)(2,1)S(1)}, f32[128,128]{1,0:T(8,128)S(1)}) custom-call(s32[320]{0:T(512)S(1)} %reduce.rows, s32[320]{0:T(512)S(1)} %reduce.1.cols, s32[1]{0:T(128)} %bitcast.7.live, bf16[32,128,128]{2,1,0:T(8,128)(2,1)S(1)} %copy-done, bf16[32,128,128]{2,1,0:T(8,128)(2,1)S(1)} %copy-done.1, ...), custom_call_target="tpu_custom_call" | custom-call | tf_op jit(solution)/shard_map/tile_products/pallas_call | solution.py:246
  38.3 0.0 copy-start.2
  38.3 1.0 %copy-done.2 = bf16[32,128,128]{2,1,0:T(8,128)(2,1)} copy-done((bf16[32,128,128]{2,1,0:T(8,128)(2,1)}, bf16[32,128,128]{2,1,0:T(8,128)(2,1)S(1)}, u32[]{:S(2)}) %copy-start.2) | copy-done | bytes 1048600
  39.2 0.0 copy-start.3
  39.2 1.0 %copy-done.3 = bf16[32,128,128]{2,1,0:T(8,128)(2,1)} copy-done((bf16[32,128,128]{2,1,0:T(8,128)(2,1)}, bf16[32,128,128]{2,1,0:T(8,128)(2,1)S(1)}, u32[]{:S(2)}) %copy-start.3) | copy-done | bytes 1048600
  40.3 0.0 copy-start.5
  40.3 0.6 copy-done.5
  40.9 37.4 %scatter_both.1 = (bf16[2,128,128]{2,1,0:T(8,128)(2,1)}, f32[128,128]{1,0:T(8,128)}, bf16[2,128,128]{2,1,0:T(8,128)(2,1)}) custom-call(bf16[32,128,128]{2,1,0:T(8,128)(2,1)} %copy-done.2, bf16[8,2,2,128,128]{4,3,2,1,0:T(8,128)(2,1)} %bitcast.8, f32[128,128]{1,0:T(8,128)} %copy-done.5, bf16[128,128]{1,0:T(8,128)(2,1)} %w_ref.3), custom_call_target="tpu_custom_call" | custom-call | tf_op jit(solution)/shard_map/scatter_both/pallas_call | solution.py:446
  78.3 1.5 %copy.14 = bf16[1,256,128]{2,1,0:T(8,128)(2,1)} copy(bf16[1,256,128]{2,1,0:T(8,128)(2,1)} %bitcast.13) | data formatting | bytes 131072
  79.8 1.5 %copy.15 = f32[128,128]{1,0:T(8,128)} copy(f32[128,128]{1,0:T(8,128)} %get-tuple-element.23) | data formatting | bytes 131072
  81.3 1.5 %copy.16 = bf16[1,256,128]{2,1,0:T(8,128)(2,1)} copy(bf16[1,256,128]{2,1,0:T(8,128)(2,1)} %bitcast.12) | data formatting | bytes 131072
Async XLA Ops:
  29.1 1.2 %copy-start = (bf16[32,128,128]{2,1,0:T(8,128)(2,1)S(1)}, bf16[32,128,128]{2,1,0:T(8,128)(2,1)}, u32[]{:S(2)}) copy-start(bf16[32,128,128]{2,1,0:T(8,128)(2,1)} %get-tuple-element.11.x_ref) | copy-start | bytes 3145732
  30.3 1.2 %copy-start.1 = (bf16[32,128,128]{2,1,0:T(8,128)(2,1)S(1)}, bf16[32,128,128]{2,1,0:T(8,128)(2,1)}, u32[]{:S(2)}) copy-start(bf16[32,128,128]{2,1,0:T(8,128)(2,1)} %get-tuple-element.12.c_ref) | copy-start | bytes 3145732
  31.6 0.8 copy-start.4
  38.3 1.0 %copy-start.2 = (bf16[32,128,128]{2,1,0:T(8,128)(2,1)}, bf16[32,128,128]{2,1,0:T(8,128)(2,1)S(1)}, u32[]{:S(2)}) copy-start(bf16[32,128,128]{2,1,0:T(8,128)(2,1)S(1)} %get-tuple-element.13.p_ref) | copy-start | bytes 3145732
  39.2 1.0 %copy-start.3 = (bf16[32,128,128]{2,1,0:T(8,128)(2,1)}, bf16[32,128,128]{2,1,0:T(8,128)(2,1)S(1)}, u32[]{:S(2)}) copy-start(bf16[32,128,128]{2,1,0:T(8,128)(2,1)S(1)} %get-tuple-element.14) | copy-start | bytes 3145732
  40.3 0.6 copy-start.5

commit v2 on v0

v2 whole, which is shorter than its diff:
```python
import functools
import math

import jax
import jax.numpy as jnp
from jax import lax
from jax.experimental import pallas as pl
from jax.experimental.pallas import tpu as pltpu
from jax.sharding import PartitionSpec as P

MESH = pl.DeviceIdType.MESH
F32 = jnp.float32
BF16 = jnp.bfloat16
I32 = jnp.int32
VM = pl.BlockSpec(memory_space=pltpu.VMEM)
LANES = 128
BLOCKS = 32
SLOTS = 320
LISTED = 384
PAIRS = (SLOTS + BLOCKS) // 2
UNROLL = 8
CHUNKS = 10
NONE = 99
FAR = 4096


def turned(row):
    return jnp.broadcast_to(row, (LANES, LANES)).T


def list_pairs(tab, base, keys, others):
    down = lax.broadcasted_iota(I32, (LANES, LANES), 0)
    across = lax.broadcasted_iota(I32, (LANES, LANES), 1)
    parts = range(len(keys))
    kc = [turned(key) for key in keys]
    xc = [turned(other) for other in others]
    count = lambda mask, what=1: jnp.sum(jnp.where(mask, what, 0), axis=0, keepdims=True)
    ranks, lows, odds = [], [], []
    for a in parts:
        rank = low = same = jnp.zeros((1, LANES), I32)
        for b in parts:
            equal = kc[b] == keys[a]
            same += count(equal)
            low += count(kc[b] < keys[a])
            if b < a:
                rank += count(equal)
            elif b == a:
                rank += count(equal & (down < across))
        ranks.append(rank)
        lows.append(low)
        odds.append(jnp.where((rank == 0) & (same % 2 == 1), 1, 0))
    oc = [turned(odd) for odd in odds]
    pc = []
    for a in parts:
        spot = ranks[a] + lows[a]
        for b in parts:
            spot += count(kc[b] < keys[a], oc[b])
        pc.append(turned(jnp.where(keys[a] >= BLOCKS, FAR, spot)))
    for q in parts:
        slot = jnp.full((1, LANES), SLOTS, I32)
        other = jnp.zeros((1, LANES), I32)
        key = jnp.full((1, LANES), NONE, I32)
        for b in parts:
            hit = pc[b] == across + q * LANES
            slot += count(hit, down + (b * LANES - SLOTS))
            other += count(hit, xc[b])
            key += count(hit, kc[b] - NONE)
        part = pl.ds(q * LANES, LANES)
        tab[base : base + 1, part] = slot
        tab[base + 1 : base + 2, part] = other
        tab[base + 2 : base + 3, part] = key
    top = jnp.zeros((1, LANES), I32)
    for b in parts:
        spots = jnp.where(kc[b] == across, pc[b] + 1, 0)
        top = jnp.maximum(top, jnp.max(spots, axis=0, keepdims=True))
    tab[base + 3 : base + 4, 0:LANES] = jnp.where(top == 0, PAIRS, (top - 1) // 2)


def make_lists(tab, pad, rows_ref, cols_ref, live):
    slot = lax.broadcasted_iota(I32, (1, SLOTS), 1)
    pad[...] = jnp.full(pad.shape, BLOCKS, I32)
    pad[0:1, 0:SLOTS] = jnp.where(slot < live, rows_ref[...], BLOCKS)
    pad[1:2, 0:SLOTS] = jnp.where(slot < live, cols_ref[...], BLOCKS)
    split = lambda i: [pad[i : i + 1, a * LANES : (a + 1) * LANES] for a in range(LISTED // LANES)]
    rows, cols = split(0), split(1)
    list_pairs(tab, 0, rows, cols)
    list_pairs(tab, 4, cols, rows)


def pair_sums(tab, base, first, last, acc, sums, product):
    def step(g, acc):
        for u in range(UNROLL):
            i = g * UNROLL + u
            a, b = 2 * i, 2 * i + 1
            made = product(tab[base, a], tab[base + 1, a], tab[base, b], tab[base + 1, b])
            before = tab[base + 2, jnp.maximum(a - 2, 0)]
            keep = (tab[base + 2, a] == before) & (i > 0)
            acc = jnp.where(keep, acc, 0.0) + made
            sums[i] = acc.astype(BF16)
        return acc

    return lax.fori_loop(first // UNROLL, last // UNROLL, step, acc)


def forward_product(v_buf, x_all, s1, c1, s2, c2):
    left = jnp.concatenate((v_buf[s1], v_buf[s2]), axis=1)
    right = jnp.concatenate((x_all[c1], x_all[c2]), axis=0)
    return jnp.dot(left, right, preferred_element_type=F32)


def backward_product(v_buf, grad_t, s1, r1, s2, r2):
    left = jnp.concatenate((grad_t[r1], grad_t[r2]), axis=1)
    right = jnp.concatenate((v_buf[s1], v_buf[s2]), axis=0)
    return jnp.dot(left, right, preferred_element_type=F32)


def place():
    r, c = lax.axis_index("row"), lax.axis_index("col")
    return r // 4, (r // 2) % 2, r % 2, c // 4, c % 4


def device(where, dy=0, dl=0, dc=0, dx=0, dz=0):
    y, l, k, x, z = where
    row = ((y + dy + 4) % 4) * 4 + ((l + dl) % 2) * 2 + (k + dc) % 2
    col = ((x + dx + 4) % 4) * 4 + (z + dz + 4) % 4
    return (row, col)


def meet(peers):
    barrier = pltpu.get_barrier_semaphore()
    for peer in peers:
        pl.semaphore_signal(barrier, inc=1, device_id=peer, device_id_type=MESH)
    pl.semaphore_wait(barrier, len(peers))


class Mail:
    def __init__(self, send_sems, recv_sems):
        self.send_sems, self.recv_sems = send_sems, recv_sems
        self.copies, self.waiting = {}, {}

    def send(self, key, src, dst, peer):
        i = len(self.copies)
        copy = pltpu.make_async_remote_copy(
            src_ref=src,
            dst_ref=dst,
            send_sem=self.send_sems.at[i],
            recv_sem=self.recv_sems.at[i],
            device_id=peer,
            device_id_type=MESH,
        )
        copy.start()
        self.copies[key] = copy
        self.waiting[key] = copy

    def take(self, *keys):
        for key in keys:
            if key in self.waiting:
                self.waiting.pop(key).wait_recv()

    def finish(self):
        self.take(*list(self.waiting))
        for copy in self.copies.values():
            copy.wait_send()


GATHER_COPIES = 6 + 24 + 1 + 10 + 8
SCATTER_COPIES = 24 + 6 + 8 + 6 + 1
GRAD_COPIES = 45
COPIES = GATHER_COPIES + SCATTER_COPIES + GRAD_COPIES
RING = ((0, 1), (1, -1), (1, 1), (0, -1))


def layer_kernel(f_ref, c_ref, w_ref, rows_ref, cols_ref, live_ref, v_hbm,
                 agg_ref, wg_ref, fg_ref,
                 f_all, c_all, v_buf, sums, grad_t, p_buf, q_buf, grad, tab, pad, tab_s,
                 xr_buf, x_buf, xs_buf, zr_buf, z_buf, zs_buf, s_buf,
                 k_buf, t_buf, y_buf, u_buf, l_buf, g1_buf, g2_buf, g3_buf,
                 v_sems, tab_sem, send_sems, recv_sems):
    per = SLOTS // CHUNKS
    loads = []
    for i in range(CHUNKS):
        part = pl.ds(i * per, per)
        loads.append(pltpu.make_async_copy(v_hbm.at[part], v_buf.at[part], v_sems.at[i]))
        loads[-1].start()

    where = place()
    y, l, k, x, z = where
    dev = functools.partial(device, where)
    xp, xm, zp, zm = dev(dx=1), dev(dx=-1), dev(dz=1), dev(dz=-1)
    yp, ym, y2, lo, other = dev(dy=1), dev(dy=-1), dev(dy=2), dev(dl=1), dev(dc=1)
    meet([xp, xm, zp, zm, yp, ym, y2, lo, other])
    mail = Mail(send_sems, recv_sems)

    def at(dx, dz):
        return ((x + dx + 4) % 4) * 4 + (z + dz + 4) % 4

    def cat(dx, dz, h):
        return c_all.at[at(dx, dz) * 2 + h]

    def fat(dy, dl):
        return f_all.at[pl.ds((((y + dy + 4) % 4) * 4 + ((l + dl) % 2) * 2 + k) * 2, 2)]

    def xsend(d, h, p):
        src = c_ref.at[h] if d == 0 else cat(0, d, h)
        mail.send(("ax", d, h, p), src, cat(0, d, h), xp if p > 0 else xm)

    def zsend(h, p):
        mail.send(("az", h, p), c_ref.at[h], cat(0, 0, h), zp if p > 0 else zm)

    def ysend(e):
        src = f_ref if e == 0 else fat(0, e)
        for dy, peer in ((1, yp), (-1, ym), (2, y2)):
            mail.send(("ay", e, dy), src, fat(0, e), peer)

    def relay(d):
        mail.take(("ax", d, 0, 1))
        mail.send(("axr", d, 1), cat(-1, d, 0), cat(-1, d, 0), xp)
        mail.take(("ax", d, 1, -1))
        mail.send(("axr", d, -1), cat(1, d, 1), cat(1, d, 1), xm)

    def share(dy, dl):
        mail.send(("ak", dy, dl), f_ref if (dy, dl) == (0, 0) else fat(dy, dl), fat(dy, dl), other)

    for h, p in RING:
        zsend(h, p)
        xsend(0, h, p)
        if (h, p) == (0, 1):
            mail.send(("al",), f_ref, fat(0, 0), lo)
    ysend(0)
    share(0, 0)
    c_all[pl.ds(at(0, 0) * 2, 2)] = c_ref[...]
    f_all[pl.ds((y * 4 + l * 2 + k) * 2, 2)] = f_ref[...]
    v_buf[SLOTS] = jnp.zeros(v_buf.shape[1:], BF16)
    sums[PAIRS] = jnp.zeros(sums.shape[1:], BF16)
    make_lists(tab, pad, rows_ref, cols_ref, live_ref[0, 0])
    to_scalars = pltpu.make_async_copy(tab, tab_s, tab_sem)
    to_scalars.start()

    mail.take(("al",))
    ysend(1)
    relay(0)
    mail.take(("az", 0, 1))
    mail.send(("azr", 1), cat(0, -1, 0), cat(0, -1, 0), zp)
    xsend(-1, 0, 1)
    xsend(-1, 0, -1)
    mail.take(("az", 1, -1))
    mail.send(("azr", -1), cat(0, 1, 1), cat(0, 1, 1), zm)
    xsend(1, 1, 1)
    xsend(1, 1, -1)
    mail.take(("az", 1, 1))
    xsend(-1, 1, 1)
    xsend(-1, 1, -1)
    mail.take(("az", 0, -1))
    xsend(1, 0, 1)
    xsend(1, 0, -1)
    share(0, 1)
    for dy in (1, -1, 2):
        mail.take(("ay", 0, dy))
        share(-dy, 0)
    relay(-1)
    mail.take(("azr", 1))
    xsend(2, 0, 1)
    xsend(2, 0, -1)
    mail.take(("azr", -1))
    xsend(2, 1, 1)
    xsend(2, 1, -1)
    relay(1)
    for dy in (1, -1, 2):
        mail.take(("ay", 1, dy))
        share(-dy, 1)
    to_scalars.wait()
    for load in loads:
        load.wait()
    mail.take(*[key for key in list(mail.waiting) if key[0] == "ak"])

    zero = jnp.zeros((LANES, LANES), F32)
    fwd = functools.partial(forward_product, v_buf, f_all)
    acc = pair_sums(tab_s, 0, 0, FIRST, zero, sums, fwd)
    relay(2)
    pair_sums(tab_s, 0, FIRST, PAIRS, acc, sums, fwd)

    def pat(dx, dz, h):
        return p_buf.at[at(dx, dz) * 2 + h]

    def chip(dy, dl):
        return ((y + dy + 4) % 4) * 2 + (l + dl) % 2

    def add(*refs):
        total = refs[0][...].astype(F32)
        for ref in refs[1:]:
            total = total + ref[...].astype(F32)
        return total

    def xrelay(d):
        i = d % 4
        mail.send(("xr", d, 1), pat(2, d, 0), xr_buf.at[i, 0], xp)
        mail.send(("xr", d, -1), pat(2, d, 1), xr_buf.at[i, 1], xm)

    def xplain(d):
        i = d % 4
        mail.send(("x", d, 1, 1), pat(1, d, 1), x_buf.at[i, 0, 1], xp)
        mail.send(("x", d, 0, -1), pat(-1, d, 0), x_buf.at[i, 1, 0], xm)

    def xsum(d):
        i = d % 4
        mail.take(("xr", d, 1))
        xs_buf[i, 0] = add(pat(1, d, 0), xr_buf.at[i, 0]).astype(BF16)
        mail.send(("x", d, 0, 1), xs_buf.at[i, 0], x_buf.at[i, 0, 0], xp)
        mail.take(("xr", d, -1))
        xs_buf[i, 1] = add(pat(-1, d, 1), xr_buf.at[i, 1]).astype(BF16)
        mail.send(("x", d, 1, -1), xs_buf.at[i, 1], x_buf.at[i, 1, 1], xm)

    def xtotal(d, h):
        i = d % 4
        mail.take(("x", d, h, 1), ("x", d, h, -1))
        return add(pat(0, d, h), x_buf.at[i, 0, h], x_buf.at[i, 1, h])

    def ksend(dy, dl):
        i = chip(dy, dl)
        mail.send(("k", dy, dl), q_buf.at[i, (k + 1) % 2], k_buf.at[i], other)

    def ktake(dy, dl):
        i = chip(dy, dl)
        mail.take(("k", dy, dl))
        t_buf[i] = add(q_buf.at[i, k], k_buf.at[i]).astype(BF16)

    def yscatter(e, dy, peer):
        mail.send(("y", e, dy), t_buf.at[chip(dy, e)], y_buf.at[e, dy % 4 - 1], peer)

    def ytotal(e):
        for dy in (1, -1, 2):
            mail.take(("y", e, dy))
        return add(t_buf.at[chip(0, e)], *[y_buf.at[e, i] for i in range(3)])

    for r in range(BLOCKS):
        p_buf[r] = sums[tab_s[3, r]]
    for d in (2, 1, -1, 0):
        xrelay(d)
    xplain(2)

    mail.take(*[key for key in list(mail.waiting) if key[0] in ("ax", "axr")])
    total = zero
    weight = w_ref[...]
    for r in range(BLOCKS):
        total += lax.dot_general(
            p_buf[r], c_all[r], (((0,), (0,)), ((), ())), preferred_element_type=F32
        )
    for i in range(16):
        grad[i] = total[8 * i : 8 * i + 8]
    g_row, g_col = y * 4 + l * 2 + k, x * 4 + z
    g1_buf[g_row] = grad[g_row]
    others = [(dy, dl, dc) for dy in range(4) for dl in range(2) for dc in range(2)][1:]
    for dy, dl, dc in others:
        to = ((y + dy) % 4) * 4 + ((l + dl) % 2) * 2 + (k + dc) % 2
        mail.send(("g1", dy, dl, dc), grad.at[to], g1_buf.at[g_row], dev(dy=dy, dl=dl, dc=dc))
    for r in range(BLOCKS):
        grad_t[r] = lax.dot_general(
            weight, c_all[r], (((1,), (1,)), ((), ())), preferred_element_type=F32
        ).astype(BF16)

    bwd = functools.partial(backward_product, v_buf, grad_t)
    acc = pair_sums(tab_s, 4, 0, FIRST, zero, sums, bwd)
    xsum(2)
    xplain(1)
    mail.take(*[("g1", *o) for o in others])
    g2_buf[g_col] = functools.reduce(jnp.add, [g1_buf[i] for i in range(16)])
    far = [(dx, dz) for dx in range(4) for dz in range(4)][1:]
    for dx, dz in far:
        mail.send(("g2", dx, dz), g2_buf.at[g_col], g2_buf.at[g_col], dev(dx=dx, dz=dz))
    xsum(1)
    xplain(-1)
    pair_sums(tab_s, 4, FIRST, PAIRS, acc, sums, bwd)

    for c in range(BLOCKS):
        q_buf[c // 4, (c // 2) % 2, c % 2] = sums[tab_s[7, c]].astype(F32).T.astype(BF16)
    for dl in (1, 0):
        for dy in (2, 1, -1, 0):
            ksend(dy, dl)
    xsum(-1)
    xplain(0)
    xsum(0)
    for e in (1, 0):
        for dy, peer in ((2, y2), (1, yp), (-1, ym)):
            ktake(dy, e)
            yscatter(e, dy, peer)
        ktake(0, e)

    s_buf[2, 0] = xtotal(2, 0).astype(BF16)
    mail.send(("zr", 1), s_buf.at[2, 0], zr_buf.at[0], zp)
    s_buf[2, 1] = xtotal(2, 1).astype(BF16)
    mail.send(("zr", -1), s_buf.at[2, 1], zr_buf.at[1], zm)
    s_buf[1, 1] = xtotal(1, 1).astype(BF16)
    mail.send(("z", 1, 1), s_buf.at[1, 1], z_buf.at[0, 1], zp)
    s_buf[3, 0] = xtotal(-1, 0).astype(BF16)
    mail.send(("z", 0, -1), s_buf.at[3, 0], z_buf.at[1, 0], zm)
    mail.take(*[("g2", *o) for o in far])
    g3_buf[g_row] = functools.reduce(jnp.add, [g2_buf[i] for i in range(16)])
    for dy, dl, dc in others:
        mail.send(("g3", dy, dl, dc), g3_buf.at[g_row], g3_buf.at[g_row], dev(dy=dy, dl=dl, dc=dc))
    total = xtotal(1, 0)
    mail.take(("zr", 1))
    zs_buf[0] = (total + zr_buf[0].astype(F32)).astype(BF16)
    mail.send(("z", 0, 1), zs_buf.at[0], z_buf.at[0, 0], zp)
    total = xtotal(-1, 1)
    mail.take(("zr", -1))
    zs_buf[1] = (total + zr_buf[1].astype(F32)).astype(BF16)
    mail.send(("z", 1, -1), zs_buf.at[1], z_buf.at[1, 1], zm)

    u_buf[...] = ytotal(1).astype(BF16)
    mail.send(("l",), u_buf, l_buf, lo)
    mine = ytotal(0)
    for h in range(2):
        total = xtotal(0, h)
        mail.take(("z", h, 1), ("z", h, -1))
        agg_ref[h] = (total + z_buf[0, h].astype(F32) + z_buf[1, h].astype(F32)).astype(BF16)
    mail.take(*[("g3", *o) for o in others])
    for i in range(16):
        wg_ref[8 * i : 8 * i + 8] = g3_buf[i]
    mail.take(("l",))
    fg_ref[...] = (mine + l_buf[...].astype(F32)).astype(BF16)
    mail.finish()


FIRST = 11 * UNROLL


def layer(features, cotangent, weight, rows, cols, live, values):
    b = (LANES, LANES)
    blocks = lambda *lead: pltpu.VMEM((*lead, *b), BF16)
    own = jax.ShapeDtypeStruct((2, *b), BF16)
    piece = pltpu.VMEM((16, 8, LANES), F32)
    return pl.pallas_call(
        layer_kernel,
        out_shape=(own, jax.ShapeDtypeStruct(b, F32), own),
        in_specs=[VM, VM, VM, VM, VM, pl.BlockSpec(memory_space=pltpu.SMEM), pl.BlockSpec(memory_space=pl.ANY)],
        out_specs=(VM,) * 3,
        scratch_shapes=[
            blocks(BLOCKS), blocks(BLOCKS), blocks(SLOTS + 1), blocks(PAIRS + 1), blocks(BLOCKS),
            blocks(BLOCKS), blocks(8, 2, 2), piece,
            pltpu.VMEM((8, LISTED), I32), pltpu.VMEM((8, LISTED), I32), pltpu.SMEM((8, LISTED), I32),
            blocks(4, 2), blocks(4, 2, 2), blocks(4, 2), blocks(2), blocks(2, 2), blocks(2), blocks(4, 2),
            blocks(8, 2), blocks(8, 2), blocks(2, 3, 2), blocks(2), blocks(2),
            piece, piece, piece,
            pltpu.SemaphoreType.DMA((CHUNKS,)), pltpu.SemaphoreType.DMA(()),
            pltpu.SemaphoreType.DMA((COPIES,)), pltpu.SemaphoreType.DMA((COPIES,)),
        ],
        compiler_params=pltpu.CompilerParams(
            collective_id=0, has_side_effects=True, vmem_limit_bytes=48 * 1024 * 1024
        ),
        name="layer",
    )(features, cotangent, weight, rows, cols, live, values)


def finish_kernel(scale, agg_ref, w_ref, g_ref, fg_ref, out_ref, wg_ref, f_ref):
    out_ref[...] = jnp.dot(agg_ref[...], w_ref[...], preferred_element_type=F32).astype(BF16)
    wg_ref[...] = g_ref[...] * scale
    f_ref[...] = fg_ref[...]


def finish(agg, weight, grad, fgrad, scale):
    shapes = [jax.ShapeDtypeStruct(a.shape, a.dtype) for a in (agg, grad, fgrad)]
    return pl.pallas_call(
        functools.partial(finish_kernel, scale),
        out_shape=shapes,
        in_specs=[VM] * 4,
        out_specs=[VM] * 3,
        name="finish",
    )(agg, weight, grad, fgrad)


def local(features, block_values, block_row, block_col, block_occupancy, weight, cotangent):
    width = features.shape[2]
    block = block_values.shape[3]
    nodes = lax.axis_size("row") * lax.axis_size("col") * features.shape[1]
    agg, grad, fgrad = layer(
        features.reshape(-1, block, width), cotangent.reshape(-1, block, width), weight,
        block_row[0], block_col[0], block_occupancy, block_values[0, 0],
    )
    out, wgrad, fgrad = finish(
        agg.reshape(-1, width), weight, grad, fgrad.reshape(-1, width), 1.0 / math.sqrt(nodes)
    )
    return (out.reshape(features.shape), wgrad, fgrad.reshape(features.shape))


def solution(mesh):
    in_specs = (
        P("col", "row", None),
        P("row", "col", None, None, None),
        P("row", "col", None),
        P("row", "col", None),
        P("row", "col"),
        P(),
        P("row", "col", None),
    )
    out_specs = (P("row", "col", None), P(), P("col", "row", None))
    return jax.shard_map(local, mesh=mesh, in_specs=in_specs, out_specs=out_specs, check_vma=False)
```

time: 500 us -> 59.1 us (0.12)
  waiting for transfers between devices: 253 us -> 0 us
  other arithmetic: 88.4 us -> 0 us
  local copies, waits for them, and re-layouts: 68.9 us -> 5.65 us
  Pallas kernels: 0 us -> 51.8 us
  matrix products: 33.7 us -> 0 us
  blocking collectives: 30.6 us -> 0 us
  between operations: 14.5 us -> 1.31 us
  starting transfers between devices: 7.63 us -> 0 us
    psum x1 -> x0, waiting for transfers between devices: 241 us -> none  [local(): lax.psum(local_grad, ('row', 'col')) * (1.0 / math.sqrt(node_total))]
    scatter-add x2 -> x0, other arithmetic: 83.8 us -> none  [the longest x1 41.9 us: local(): grad_partial = jnp.zeros((col_blocks, block_size, feature_width), jnp.flo...]
    pallas_call x0 -> x2, Pallas kernels: none -> 51.8 us  [the longest x1 50.1 us: layer(): pl.pallas_call(layer_kernel, out_shape=(own, jax.ShapeDtypeStruct(b, F32)...]
    dot_general x2 -> x0, local copies, waits for them, and re-layouts: 42.3 us -> none  [the longest x1 21.2 us: local(): jnp.einsum('sab,saf->sbf', values, grad_picked, preferred_element_type=jn...]
    dot_general x5 -> x0, matrix products: 33.7 us -> none  [the longest x1 15.5 us: local(): jnp.einsum('sab,sbf->saf', values, picked, preferred_element_type=jnp.flo...]
    all_to_all x1 -> x0, blocking collectives: 30.6 us -> none  [summed_on_arrival(): lax.all_to_all(blocks, axis, split_axis=0, concat_axis=0, tiled=True)]
    gather x2 -> x0, local copies, waits for them, and re-layouts: 22.7 us -> none  [the longest x1 12 us: local(): grad_rows.reshape(row_block_indices, block_size, feature_width)]
    all_to_all x1 -> x0, waiting for transfers between devices: 12.6 us -> none  [from_everyone(): lax.all_to_all(jnp.broadcast_to(array[None], (length, *array.shape)), axi...]
  transfers between devices with their start and end apart: 4 -> 0, of which waited for: 2 -> 0; matrix products, arithmetic and copies ran while one was open for 37% -> 0% of each run, Pallas kernels for 0% -> 0%
where the time goes in v2:
time: 59.1 us; the launch traced here: 58.8 us
  Pallas kernels  51.8 us (88%)
  local copies, waits for them, and re-layouts  5.65 us (10%)
  between operations  1.31 us (2%)
    pallas_call x1, Pallas kernels, layer(): pl.pallas_call(layer_kernel, out_shape=(own, jax.ShapeDtypeStruct(b, F32)...  50.1 us
    unnamed x16, local copies, waits for them, and re-layouts  5.65 us
    pallas_call x1, Pallas kernels, finish(): pl.pallas_call(functools.partial(finish_kernel, scale), out_shape=shapes,...  1.7 us

profile of v2, /device:TPU:1, one launch (start us, length us, event | category | flops | bytes accessed | tf_op | source)
XLA Modules:
  0.0 58.8 jit_solution(8131452067518034908)
XLA Ops:
  1.3 0.0 copy-start
  1.3 0.7 %copy-done = bf16[128,128]{1,0:T(8,128)(2,1)S(1)} copy-done((bf16[128,128]{1,0:T(8,128)(2,1)S(1)}, bf16[128,128]{1,0:T(8,128)(2,1)}, u32[]{:S(2)}) %copy-start) | copy-done | bytes 32792
  2.0 0.0 copy-start.1
  2.0 0.8 %copy-done.1 = bf16[1,256,128]{2,1,0:T(8,128)(2,1)S(1)} copy-done((bf16[1,256,128]{2,1,0:T(8,128)(2,1)S(1)}, bf16[1,256,128]{2,1,0:T(8,128)(2,1)}, u32[]{:S(2)}) %copy-start.1) | copy-done | bytes 65560
  2.9 0.0 copy-start.2
  2.9 0.8 %copy-done.2 = bf16[1,256,128]{2,1,0:T(8,128)(2,1)S(1)} copy-done((bf16[1,256,128]{2,1,0:T(8,128)(2,1)S(1)}, bf16[1,256,128]{2,1,0:T(8,128)(2,1)}, u32[]{:S(2)}) %copy-start.2) | copy-done | bytes 65560
  3.7 0.0 copy-start.6
  3.7 0.7 %copy-done.6 = s32[1,1,320]{2,1,0:T(1,128)S(1)} copy-done((s32[1,1,320]{2,1,0:T(1,128)S(1)}, s32[1,1,320]{2,1,0:T(1,128)}, u32[]{:S(2)}) %copy-start.6) | copy-done | bytes 1304
  4.4 0.0 copy-start.7
  4.4 0.7 %copy-done.7 = s32[1,1,320]{2,1,0:T(1,128)S(1)} copy-done((s32[1,1,320]{2,1,0:T(1,128)S(1)}, s32[1,1,320]{2,1,0:T(1,128)}, u32[]{:S(2)}) %copy-start.7) | copy-done | bytes 1304
  5.1 50.1 %layer.1 = (bf16[2,128,128]{2,1,0:T(8,128)(2,1)S(1)}, f32[128,128]{1,0:T(8,128)S(1)}, bf16[2,128,128]{2,1,0:T(8,128)(2,1)S(1)}) custom-call(bf16[2,128,128]{2,1,0:T(8,128)(2,1)S(1)} %bitcast.9, bf16[2,128,128]{2,1,0:T(8,128)(2,1)S(1)} %bitcast.10, bf16[128,128]{1,0:T(8,128)(2,1)S(1)} %copy-done, s32[1,320]{1,0:T(1,128)S(1)} %bitcast.13, ...), custom_call_target="tpu_custom_call" | custom-call | tf_op jit(solution)/shard_map/layer/pallas_call | solution.py:432
  55.2 0.0 copy-start.3
  55.2 0.6 %copy-done.3 = bf16[2,128,128]{2,1,0:T(8,128)(2,1)} copy-done((bf16[2,128,128]{2,1,0:T(8,128)(2,1)}, bf16[2,128,128]{2,1,0:T(8,128)(2,1)S(1)}, u32[]{:S(2)}) %copy-start.3) | copy-done | bytes 65560
  55.8 0.0 copy-start.4
  55.8 0.6 %copy-done.4 = f32[128,128]{1,0:T(8,128)} copy-done((f32[128,128]{1,0:T(8,128)}, f32[128,128]{1,0:T(8,128)S(1)}, u32[]{:S(2)}) %copy-start.4) | copy-done | bytes 65560
  56.4 0.0 copy-start.5
  56.4 0.6 %copy-done.5 = bf16[2,128,128]{2,1,0:T(8,128)(2,1)} copy-done((bf16[2,128,128]{2,1,0:T(8,128)(2,1)}, bf16[2,128,128]{2,1,0:T(8,128)(2,1)S(1)}, u32[]{:S(2)}) %copy-start.5) | copy-done | bytes 65560
  57.0 1.7 %finish.1 = (bf16[256,128]{1,0:T(8,128)(2,1)}, f32[128,128]{1,0:T(8,128)}, bf16[256,128]{1,0:T(8,128)(2,1)}) custom-call(bf16[256,128]{1,0:T(8,128)(2,1)} %bitcast.11, bf16[128,128]{1,0:T(8,128)(2,1)} %w_ref.3, f32[128,128]{1,0:T(8,128)} %copy-done.4, bf16[256,128]{1,0:T(8,128)(2,1)} %bitcast.12), custom_call_target="tpu_custom_call" | custom-call | tf_op jit(solution)/shard_map/finish/pallas_call | solution.py:462
Async XLA Ops:
  1.3 0.8 %copy-start = (bf16[128,128]{1,0:T(8,128)(2,1)S(1)}, bf16[128,128]{1,0:T(8,128)(2,1)}, u32[]{:S(2)}) copy-start(bf16[128,128]{1,0:T(8,128)(2,1)} %w_ref.3) | copy-start | bytes 98308
  2.0 0.8 %copy-start.1 = (bf16[1,256,128]{2,1,0:T(8,128)(2,1)S(1)}, bf16[1,256,128]{2,1,0:T(8,128)(2,1)}, u32[]{:S(2)}) copy-start(bf16[1,256,128]{2,1,0:T(8,128)(2,1)} %param.7) | copy-start | bytes 196612
  2.9 0.8 %copy-start.2 = (bf16[1,256,128]{2,1,0:T(8,128)(2,1)S(1)}, bf16[1,256,128]{2,1,0:T(8,128)(2,1)}, u32[]{:S(2)}) copy-start(bf16[1,256,128]{2,1,0:T(8,128)(2,1)} %param.13) | copy-start | bytes 196612
  3.7 0.7 %copy-start.6 = (s32[1,1,320]{2,1,0:T(1,128)S(1)}, s32[1,1,320]{2,1,0:T(1,128)}, u32[]{:S(2)}) copy-start(s32[1,1,320]{2,1,0:T(1,128)} %param.9) | copy-start | bytes 3844
  4.4 0.7 %copy-start.7 = (s32[1,1,320]{2,1,0:T(1,128)S(1)}, s32[1,1,320]{2,1,0:T(1,128)}, u32[]{:S(2)}) copy-start(s32[1,1,320]{2,1,0:T(1,128)} %param.10) | copy-start | bytes 3844
  55.2 0.6 %copy-start.3 = (bf16[2,128,128]{2,1,0:T(8,128)(2,1)}, bf16[2,128,128]{2,1,0:T(8,128)(2,1)S(1)}, u32[]{:S(2)}) copy-start(bf16[2,128,128]{2,1,0:T(8,128)(2,1)S(1)} %get-tuple-element.9) | copy-start | bytes 196612
  55.8 0.6 %copy-start.4 = (f32[128,128]{1,0:T(8,128)}, f32[128,128]{1,0:T(8,128)S(1)}, u32[]{:S(2)}) copy-start(f32[128,128]{1,0:T(8,128)S(1)} %get-tuple-element.10.g_ref) | copy-start | bytes 196612
  56.4 0.6 %copy-start.5 = (bf16[2,128,128]{2,1,0:T(8,128)(2,1)}, bf16[2,128,128]{2,1,0:T(8,128)(2,1)S(1)}, u32[]{:S(2)}) copy-start(bf16[2,128,128]{2,1,0:T(8,128)(2,1)S(1)} %get-tuple-element.11) | copy-start | bytes 196612

commit v3 on v2

--- a/solution.py
+++ b/solution.py
@@ -13,6 +13,7 @@
 BF16 = jnp.bfloat16
 I32 = jnp.int32
 VM = pl.BlockSpec(memory_space=pltpu.VMEM)
+ANY = pl.BlockSpec(memory_space=pltpu.HBM)
 LANES = 128
 BLOCKS = 32
 SLOTS = 320
@@ -170,26 +171,33 @@
 RING = ((0, 1), (1, -1), (1, 1), (0, -1))
 
 
-def layer_kernel(f_ref, c_ref, w_ref, rows_ref, cols_ref, live_ref, v_hbm,
+def layer_kernel(f_hbm, c_hbm, w_hbm, rows_hbm, cols_hbm, live_ref, v_hbm,
                  agg_ref, wg_ref, fg_ref,
-                 f_all, c_all, v_buf, sums, grad_t, p_buf, q_buf, grad, tab, pad, tab_s,
+                 w_ref, rows_ref, cols_ref, f_all, c_all, v_buf, sums, grad_t, p_buf, q_buf, grad, tab, pad, tab_s,
                  xr_buf, x_buf, xs_buf, zr_buf, z_buf, zs_buf, s_buf,
                  k_buf, t_buf, y_buf, u_buf, l_buf, g1_buf, g2_buf, g3_buf,
-                 v_sems, tab_sem, send_sems, recv_sems):
+                 in_sems, v_sems, tab_sem, send_sems, recv_sems):
+    where = place()
+    y, l, k, x, z = where
+    g_row, g_col = y * 4 + l * 2 + k, x * 4 + z
+    f_own, c_own = f_all.at[pl.ds(g_row * 2, 2)], c_all.at[pl.ds(g_col * 2, 2)]
+    pairs = ((c_hbm, c_own), (f_hbm, f_own), (rows_hbm, rows_ref), (cols_hbm, cols_ref), (w_hbm, w_ref))
+    inputs = [pltpu.make_async_copy(src, dst, in_sems.at[i]) for i, (src, dst) in enumerate(pairs)]
+    for copy in inputs:
+        copy.start()
     per = SLOTS // CHUNKS
     loads = []
     for i in range(CHUNKS):
         part = pl.ds(i * per, per)
         loads.append(pltpu.make_async_copy(v_hbm.at[part], v_buf.at[part], v_sems.at[i]))
         loads[-1].start()
-
-    where = place()
-    y, l, k, x, z = where
     dev = functools.partial(device, where)
     xp, xm, zp, zm = dev(dx=1), dev(dx=-1), dev(dz=1), dev(dz=-1)
     yp, ym, y2, lo, other = dev(dy=1), dev(dy=-1), dev(dy=2), dev(dl=1), dev(dc=1)
     meet([xp, xm, zp, zm, yp, ym, y2, lo, other])
     mail = Mail(send_sems, recv_sems)
+    for copy in inputs:
+        copy.wait()
 
     def at(dx, dz):
         return ((x + dx + 4) % 4) * 4 + (z + dz + 4) % 4
@@ -201,16 +209,14 @@
         return f_all.at[pl.ds((((y + dy + 4) % 4) * 4 + ((l + dl) % 2) * 2 + k) * 2, 2)]
 
     def xsend(d, h, p):
-        src = c_ref.at[h] if d == 0 else cat(0, d, h)
-        mail.send(("ax", d, h, p), src, cat(0, d, h), xp if p > 0 else xm)
+        mail.send(("ax", d, h, p), cat(0, d, h), cat(0, d, h), xp if p > 0 else xm)
 
     def zsend(h, p):
-        mail.send(("az", h, p), c_ref.at[h], cat(0, 0, h), zp if p > 0 else zm)
+        mail.send(("az", h, p), cat(0, 0, h), cat(0, 0, h), zp if p > 0 else zm)
 
     def ysend(e):
-        src = f_ref if e == 0 else fat(0, e)
         for dy, peer in ((1, yp), (-1, ym), (2, y2)):
-            mail.send(("ay", e, dy), src, fat(0, e), peer)
+            mail.send(("ay", e, dy), fat(0, e), fat(0, e), peer)
 
     def relay(d):
         mail.take(("ax", d, 0, 1))
@@ -219,17 +225,15 @@
         mail.send(("axr", d, -1), cat(1, d, 1), cat(1, d, 1), xm)
 
     def share(dy, dl):
-        mail.send(("ak", dy, dl), f_ref if (dy, dl) == (0, 0) else fat(dy, dl), fat(dy, dl), other)
+        mail.send(("ak", dy, dl), fat(dy, dl), fat(dy, dl), other)
 
     for h, p in RING:
         zsend(h, p)
         xsend(0, h, p)
         if (h, p) == (0, 1):
-            mail.send(("al",), f_ref, fat(0, 0), lo)
+            mail.send(("al",), fat(0, 0), fat(0, 0), lo)
     ysend(0)
     share(0, 0)
-    c_all[pl.ds(at(0, 0) * 2, 2)] = c_ref[...]
-    f_all[pl.ds((y * 4 + l * 2 + k) * 2, 2)] = f_ref[...]
     v_buf[SLOTS] = jnp.zeros(v_buf.shape[1:], BF16)
     sums[PAIRS] = jnp.zeros(sums.shape[1:], BF16)
     make_lists(tab, pad, rows_ref, cols_ref, live_ref[0, 0])
@@ -347,7 +351,6 @@
         )
     for i in range(16):
         grad[i] = total[8 * i : 8 * i + 8]
-    g_row, g_col = y * 4 + l * 2 + k, x * 4 + z
     g1_buf[g_row] = grad[g_row]
     others = [(dy, dl, dc) for dy in range(4) for dl in range(2) for dc in range(2)][1:]
     for dy, dl, dc in others:
@@ -432,20 +435,21 @@
     return pl.pallas_call(
         layer_kernel,
         out_shape=(own, jax.ShapeDtypeStruct(b, F32), own),
-        in_specs=[VM, VM, VM, VM, VM, pl.BlockSpec(memory_space=pltpu.SMEM), pl.BlockSpec(memory_space=pl.ANY)],
+        in_specs=[ANY, ANY, ANY, ANY, ANY, pl.BlockSpec(memory_space=pltpu.SMEM), ANY],
         out_specs=(VM,) * 3,
         scratch_shapes=[
+            pltpu.VMEM(b, BF16), pltpu.VMEM((1, SLOTS), I32), pltpu.VMEM((1, SLOTS), I32),
             blocks(BLOCKS), blocks(BLOCKS), blocks(SLOTS + 1), blocks(PAIRS + 1), blocks(BLOCKS),
             blocks(BLOCKS), blocks(8, 2, 2), piece,
             pltpu.VMEM((8, LISTED), I32), pltpu.VMEM((8, LISTED), I32), pltpu.SMEM((8, LISTED), I32),
             blocks(4, 2), blocks(4, 2, 2), blocks(4, 2), blocks(2), blocks(2, 2), blocks(2), blocks(4, 2),
             blocks(8, 2), blocks(8, 2), blocks(2, 3, 2), blocks(2), blocks(2),
             piece, piece, piece,
-            pltpu.SemaphoreType.DMA((CHUNKS,)), pltpu.SemaphoreType.DMA(()),
+            pltpu.SemaphoreType.DMA((5,)), pltpu.SemaphoreType.DMA((CHUNKS,)), pltpu.SemaphoreType.DMA(()),
             pltpu.SemaphoreType.DMA((COPIES,)), pltpu.SemaphoreType.DMA((COPIES,)),
         ],
         compiler_params=pltpu.CompilerParams(
-            collective_id=0, has_side_effects=True, vmem_limit_bytes=48 * 1024 * 1024
+            collective_id=0, has_side_effects=True, vmem_limit_bytes=67043328
         ),
         name="layer",
     )(features, cotangent, weight, rows, cols, live, values)
@@ -464,6 +468,7 @@
         out_shape=shapes,
         in_specs=[VM] * 4,
         out_specs=[VM] * 3,
+        compiler_params=pltpu.CompilerParams(vmem_limit_bytes=67043328),
         name="finish",
     )(agg, weight, grad, fgrad)
 

time: 59.1 us -> 55.9 us (0.946)
  local copies, waits for them, and re-layouts: 5.65 us -> 0 us
  Pallas kernels: 51.8 us -> 54.5 us
    unnamed x16 -> x0, local copies, waits for them, and re-layouts: 5.65 us -> none
    pallas_call x1, Pallas kernels: 50.1 us -> 52.8 us  [layer(): pl.pallas_call(layer_kernel, out_shape=(own, jax.ShapeDtypeStruct(b, F32)...]
where the time goes in v3:
time: 55.9 us; the launch traced here: 55.8 us
  Pallas kernels  54.5 us (97%)
  between operations  1.29 us (2%)
    pallas_call x1, Pallas kernels, layer(): pl.pallas_call(layer_kernel, out_shape=(own, jax.ShapeDtypeStruct(b, F32)...  52.8 us
    pallas_call x1, Pallas kernels, finish(): pl.pallas_call(functools.partial(finish_kernel, scale), out_shape=shapes,...  1.71 us

profile of v3, /device:TPU:1, one launch (start us, length us, event | category | flops | bytes accessed | tf_op | source)
XLA Modules:
  0.0 55.8 jit_solution(18112016287738748378)
XLA Ops:
  1.3 52.8 %layer.1 = (bf16[2,128,128]{2,1,0:T(8,128)(2,1)}, f32[128,128]{1,0:T(8,128)}, bf16[2,128,128]{2,1,0:T(8,128)(2,1)}) custom-call(bf16[2,128,128]{2,1,0:T(8,128)(2,1)} %bitcast.10, bf16[2,128,128]{2,1,0:T(8,128)(2,1)} %bitcast.11, bf16[128,128]{1,0:T(8,128)(2,1)} %w_ref.1, s32[1,320]{1,0:T(1,128)} %bitcast.14, s32[1,320]{1,0:T(1,128)} %bitcast.15, ...), custom_call_target="tpu_custom_call" | custom-call | tf_op jit(solution)/shard_map/layer/pallas_call | solution.py:435
  54.0 1.7 %finish.1 = (bf16[256,128]{1,0:T(8,128)(2,1)}, f32[128,128]{1,0:T(8,128)}, bf16[256,128]{1,0:T(8,128)(2,1)}) custom-call(bf16[256,128]{1,0:T(8,128)(2,1)} %bitcast.12, bf16[128,128]{1,0:T(8,128)(2,1)} %w_ref.1, f32[128,128]{1,0:T(8,128)} %get-tuple-element.10.g_ref, bf16[256,128]{1,0:T(8,128)(2,1)} %bitcast.13), custom_call_target="tpu_custom_call" | custom-call | tf_op jit(solution)/shard_map/finish/pallas_call | solution.py:466

commit v4 on v3

--- a/solution.py
+++ b/solution.py
@@ -77,15 +77,14 @@
     tab[base + 3 : base + 4, 0:LANES] = jnp.where(top == 0, PAIRS, (top - 1) // 2)
 
 
-def make_lists(tab, pad, rows_ref, cols_ref, live):
+def live_keys(pad, rows_ref, cols_ref, live):
     slot = lax.broadcasted_iota(I32, (1, SLOTS), 1)
     pad[...] = jnp.full(pad.shape, BLOCKS, I32)
     pad[0:1, 0:SLOTS] = jnp.where(slot < live, rows_ref[...], BLOCKS)
     pad[1:2, 0:SLOTS] = jnp.where(slot < live, cols_ref[...], BLOCKS)
     split = lambda i: [pad[i : i + 1, a * LANES : (a + 1) * LANES] for a in range(LISTED // LANES)]
     rows, cols = split(0), split(1)
-    list_pairs(tab, 0, rows, cols)
-    list_pairs(tab, 4, cols, rows)
+    return rows, cols
 
 
 def pair_sums(tab, base, first, last, acc, sums, product):
@@ -137,10 +136,11 @@
 class Mail:
     def __init__(self, send_sems, recv_sems):
         self.send_sems, self.recv_sems = send_sems, recv_sems
-        self.copies, self.waiting = {}, {}
+        self.count, self.sending, self.waiting, self.bursts = 0, {}, {}, {}
 
     def send(self, key, src, dst, peer):
-        i = len(self.copies)
+        i = self.count
+        self.count += 1
         copy = pltpu.make_async_remote_copy(
             src_ref=src,
             dst_ref=dst,
@@ -150,7 +150,7 @@
             device_id_type=MESH,
         )
         copy.start()
-        self.copies[key] = copy
+        self.sending[key] = copy
         self.waiting[key] = copy
 
     def take(self, *keys):
@@ -158,25 +158,52 @@
             if key in self.waiting:
                 self.waiting.pop(key).wait_recv()
 
+    def burst(self, key, whole, items):
+        i = self.count
+        self.count += 1
+        for src, dst, peer in items:
+            pltpu.make_async_remote_copy(
+                src_ref=src,
+                dst_ref=dst,
+                send_sem=self.send_sems.at[i],
+                recv_sem=self.recv_sems.at[i],
+                device_id=peer,
+                device_id_type=MESH,
+            ).start()
+        self.bursts[key] = (i, whole.at[pl.ds(0, len(items))])
+
+    def drain(self, key):
+        i, part = self.bursts[key]
+        pltpu.make_async_copy(part, part, self.recv_sems.at[i]).wait()
+
+    def settle_bursts(self):
+        for i, part in self.bursts.values():
+            pltpu.make_async_copy(part, part, self.send_sems.at[i]).wait()
+
+    def settle(self, *kinds):
+        for key in list(self.sending):
+            if not kinds or key[0] in kinds:
+                self.sending.pop(key).wait_send()
+
     def finish(self):
         self.take(*list(self.waiting))
-        for copy in self.copies.values():
-            copy.wait_send()
-
-
-GATHER_COPIES = 6 + 24 + 1 + 10 + 8
-SCATTER_COPIES = 24 + 6 + 8 + 6 + 1
-GRAD_COPIES = 45
+        self.settle()
+        self.settle_bursts()
+
+
+GATHER_COPIES = 6 + 24 + 2 + 12 + 8
+SCATTER_COPIES = 3 + 18 + 6 + 8 + 6 + 1
+GRAD_COPIES = 3
 COPIES = GATHER_COPIES + SCATTER_COPIES + GRAD_COPIES
 RING = ((0, 1), (1, -1), (1, 1), (0, -1))
 
 
 def layer_kernel(f_hbm, c_hbm, w_hbm, rows_hbm, cols_hbm, live_ref, v_hbm,
                  agg_ref, wg_ref, fg_ref,
-                 w_ref, rows_ref, cols_ref, f_all, c_all, v_buf, sums, grad_t, p_buf, q_buf, grad, tab, pad, tab_s,
-                 xr_buf, x_buf, xs_buf, zr_buf, z_buf, zs_buf, s_buf,
+                 w_ref, rows_ref, cols_ref, f_all, c_all, v_buf, sums, grad_t, p_buf, q_buf, grad, row_tab, col_tab, pad, row_tab_s, col_tab_s,
+                 xr_buf, x_buf, xs_buf, xf_buf, zr_buf, z_buf, s_buf,
                  k_buf, t_buf, y_buf, u_buf, l_buf, g1_buf, g2_buf, g3_buf,
-                 in_sems, v_sems, tab_sem, send_sems, recv_sems):
+                 in_sems, v_sems, tab_sems, send_sems, recv_sems):
     where = place()
     y, l, k, x, z = where
     g_row, g_col = y * 4 + l * 2 + k, x * 4 + z
@@ -185,12 +212,6 @@
     inputs = [pltpu.make_async_copy(src, dst, in_sems.at[i]) for i, (src, dst) in enumerate(pairs)]
     for copy in inputs:
         copy.start()
-    per = SLOTS // CHUNKS
-    loads = []
-    for i in range(CHUNKS):
-        part = pl.ds(i * per, per)
-        loads.append(pltpu.make_async_copy(v_hbm.at[part], v_buf.at[part], v_sems.at[i]))
-        loads[-1].start()
     dev = functools.partial(device, where)
     xp, xm, zp, zm = dev(dx=1), dev(dx=-1), dev(dz=1), dev(dz=-1)
     yp, ym, y2, lo, other = dev(dy=1), dev(dy=-1), dev(dy=2), dev(dl=1), dev(dc=1)
@@ -214,9 +235,12 @@
     def zsend(h, p):
         mail.send(("az", h, p), cat(0, 0, h), cat(0, 0, h), zp if p > 0 else zm)
 
-    def ysend(e):
-        for dy, peer in ((1, yp), (-1, ym), (2, y2)):
-            mail.send(("ay", e, dy), fat(0, e), fat(0, e), peer)
+    def fhalf(dy, dl, h):
+        return f_all.at[(((y + dy + 4) % 4) * 4 + ((l + dl) % 2) * 2 + k) * 2 + h]
+
+    def ysend(e, h):
+        for dy, peer in ((2, y2), (1, yp), (-1, ym)):
+            mail.send(("ay", e, dy, h), fhalf(0, e, h), fhalf(0, e, h), peer)
 
     def relay(d):
         mail.take(("ax", d, 0, 1))
@@ -227,22 +251,32 @@
     def share(dy, dl):
         mail.send(("ak", dy, dl), fat(dy, dl), fat(dy, dl), other)
 
+    for h in range(2):
+        mail.send(("al", h), fhalf(0, 0, h), fhalf(0, 0, h), lo)
     for h, p in RING:
         zsend(h, p)
         xsend(0, h, p)
-        if (h, p) == (0, 1):
-            mail.send(("al",), fat(0, 0), fat(0, 0), lo)
-    ysend(0)
+    for h in range(2):
+        ysend(0, h)
     share(0, 0)
     v_buf[SLOTS] = jnp.zeros(v_buf.shape[1:], BF16)
     sums[PAIRS] = jnp.zeros(sums.shape[1:], BF16)
-    make_lists(tab, pad, rows_ref, cols_ref, live_ref[0, 0])
-    to_scalars = pltpu.make_async_copy(tab, tab_s, tab_sem)
-    to_scalars.start()
-
-    mail.take(("al",))
-    ysend(1)
+    rows, cols = live_keys(pad, rows_ref, cols_ref, live_ref[0, 0])
+    list_pairs(row_tab, 0, rows, cols)
+    row_scalars = pltpu.make_async_copy(row_tab, row_tab_s, tab_sems.at[0])
+    row_scalars.start()
+
+    for h in range(2):
+        mail.take(("al", h))
+        ysend(1, h)
+    share(0, 1)
     relay(0)
+    per = SLOTS // CHUNKS
+    loads = []
+    for i in range(CHUNKS):
+        part = pl.ds(i * per, per)
+        loads.append(pltpu.make_async_copy(v_hbm.at[part], v_buf.at[part], v_sems.at[i]))
+        loads[-1].start()
     mail.take(("az", 0, 1))
     mail.send(("azr", 1), cat(0, -1, 0), cat(0, -1, 0), zp)
     xsend(-1, 0, 1)
@@ -257,31 +291,31 @@
     mail.take(("az", 0, -1))
     xsend(1, 0, 1)
     xsend(1, 0, -1)
-    share(0, 1)
     for dy in (1, -1, 2):
-        mail.take(("ay", 0, dy))
+        mail.take(("ay", 0, dy, 0), ("ay", 0, dy, 1))
         share(-dy, 0)
+    list_pairs(col_tab, 0, cols, rows)
+    col_scalars = pltpu.make_async_copy(col_tab, col_tab_s, tab_sems.at[1])
+    col_scalars.start()
+    for dy in (1, -1, 2):
+        mail.take(("ay", 1, dy, 0), ("ay", 1, dy, 1))
+        share(-dy, 1)
     relay(-1)
-    mail.take(("azr", 1))
-    xsend(2, 0, 1)
-    xsend(2, 0, -1)
-    mail.take(("azr", -1))
-    xsend(2, 1, 1)
-    xsend(2, 1, -1)
     relay(1)
-    for dy in (1, -1, 2):
-        mail.take(("ay", 1, dy))
-        share(-dy, 1)
-    to_scalars.wait()
+    for h, p in ((0, 1), (1, -1)):
+        mail.take(("azr", p))
+        xsend(2, h, 1)
+        xsend(2, h, -1)
+        mail.send(("axf", h), cat(0, 2, h), cat(0, 2, h), dev(dx=2))
+    row_scalars.wait()
+    col_scalars.wait()
     for load in loads:
         load.wait()
     mail.take(*[key for key in list(mail.waiting) if key[0] == "ak"])
 
     zero = jnp.zeros((LANES, LANES), F32)
     fwd = functools.partial(forward_product, v_buf, f_all)
-    acc = pair_sums(tab_s, 0, 0, FIRST, zero, sums, fwd)
-    relay(2)
-    pair_sums(tab_s, 0, FIRST, PAIRS, acc, sums, fwd)
+    pair_sums(row_tab_s, 0, 0, PAIRS, zero, sums, fwd)
 
     def pat(dx, dz, h):
         return p_buf.at[at(dx, dz) * 2 + h]
@@ -319,6 +353,14 @@
         mail.take(("x", d, h, 1), ("x", d, h, -1))
         return add(pat(0, d, h), x_buf.at[i, 0, h], x_buf.at[i, 1, h])
 
+    def xfar():
+        for j, (dx, peer) in enumerate(((1, xp), (-1, xm), (2, dev(dx=2)))):
+            src = p_buf.at[pl.ds(at(dx, 2) * 2, 2)]
+            mail.send(("xf", dx), src, xf_buf.at[j], peer)
+
+    def zsend_half(d, h, peer):
+        mail.send(("z", d, h), s_buf.at[d % 4, h], z_buf.at[0 if d == 1 else 1, h], peer)
+
     def ksend(dy, dl):
         i = chip(dy, dl)
         mail.send(("k", dy, dl), q_buf.at[i, (k + 1) % 2], k_buf.at[i], other)
@@ -337,12 +379,14 @@
         return add(t_buf.at[chip(0, e)], *[y_buf.at[e, i] for i in range(3)])
 
     for r in range(BLOCKS):
-        p_buf[r] = sums[tab_s[3, r]]
-    for d in (2, 1, -1, 0):
-        xrelay(d)
-    xplain(2)
-
-    mail.take(*[key for key in list(mail.waiting) if key[0] in ("ax", "axr")])
+        p_buf[r] = sums[row_tab_s[3, r]]
+    xrelay(1)
+    xrelay(-1)
+    xfar()
+    xrelay(0)
+    xplain(1)
+    xplain(-1)
+    mail.take(*[key for key in list(mail.waiting) if key[0] in ("ax", "axr", "axf")])
     total = zero
     weight = w_ref[...]
     for r in range(BLOCKS):
@@ -353,70 +397,77 @@
         grad[i] = total[8 * i : 8 * i + 8]
     g1_buf[g_row] = grad[g_row]
     others = [(dy, dl, dc) for dy in range(4) for dl in range(2) for dc in range(2)][1:]
+    items = []
     for dy, dl, dc in others:
         to = ((y + dy) % 4) * 4 + ((l + dl) % 2) * 2 + (k + dc) % 2
-        mail.send(("g1", dy, dl, dc), grad.at[to], g1_buf.at[g_row], dev(dy=dy, dl=dl, dc=dc))
+        items.append((grad.at[to], g1_buf.at[g_row], dev(dy=dy, dl=dl, dc=dc)))
+    mail.burst("g1", g1_buf, items)
     for r in range(BLOCKS):
         grad_t[r] = lax.dot_general(
             weight, c_all[r], (((1,), (1,)), ((), ())), preferred_element_type=F32
         ).astype(BF16)
 
     bwd = functools.partial(backward_product, v_buf, grad_t)
-    acc = pair_sums(tab_s, 4, 0, FIRST, zero, sums, bwd)
-    xsum(2)
-    xplain(1)
-    mail.take(*[("g1", *o) for o in others])
-    g2_buf[g_col] = functools.reduce(jnp.add, [g1_buf[i] for i in range(16)])
-    far = [(dx, dz) for dx in range(4) for dz in range(4)][1:]
-    for dx, dz in far:
-        mail.send(("g2", dx, dz), g2_buf.at[g_col], g2_buf.at[g_col], dev(dx=dx, dz=dz))
+    acc = pair_sums(col_tab_s, 0, STOPS[0], STOPS[1], zero, sums, bwd)
+    acc = pair_sums(col_tab_s, 0, STOPS[1], STOPS[2], acc, sums, bwd)
     xsum(1)
-    xplain(-1)
-    pair_sums(tab_s, 4, FIRST, PAIRS, acc, sums, bwd)
+    xsum(-1)
+    xplain(0)
+    mail.take(("xf", 1), ("xf", -1), ("xf", 2))
+    far_part = p_buf.at[pl.ds(at(0, 2) * 2, 2)]
+    s_buf[2] = add(far_part, xf_buf.at[0], xf_buf.at[1], xf_buf.at[2]).astype(BF16)
+    mail.send(("zr", 1), s_buf.at[2, 0], zr_buf.at[0], zp)
+    mail.send(("zr", -1), s_buf.at[2, 1], zr_buf.at[1], zm)
+    acc = pair_sums(col_tab_s, 0, STOPS[2], STOPS[3], acc, sums, bwd)
+    xsum(0)
+    pair_sums(col_tab_s, 0, STOPS[3], STOPS[4], acc, sums, bwd)
 
     for c in range(BLOCKS):
-        q_buf[c // 4, (c // 2) % 2, c % 2] = sums[tab_s[7, c]].astype(F32).T.astype(BF16)
+        q_buf[c // 4, (c // 2) % 2, c % 2] = sums[col_tab_s[3, c]].astype(F32).T.astype(BF16)
     for dl in (1, 0):
         for dy in (2, 1, -1, 0):
             ksend(dy, dl)
-    xsum(-1)
-    xplain(0)
-    xsum(0)
-    for e in (1, 0):
-        for dy, peer in ((2, y2), (1, yp), (-1, ym)):
-            ktake(dy, e)
-            yscatter(e, dy, peer)
-        ktake(0, e)
-
-    s_buf[2, 0] = xtotal(2, 0).astype(BF16)
-    mail.send(("zr", 1), s_buf.at[2, 0], zr_buf.at[0], zp)
-    s_buf[2, 1] = xtotal(2, 1).astype(BF16)
-    mail.send(("zr", -1), s_buf.at[2, 1], zr_buf.at[1], zm)
-    s_buf[1, 1] = xtotal(1, 1).astype(BF16)
-    mail.send(("z", 1, 1), s_buf.at[1, 1], z_buf.at[0, 1], zp)
-    s_buf[3, 0] = xtotal(-1, 0).astype(BF16)
-    mail.send(("z", 0, -1), s_buf.at[3, 0], z_buf.at[1, 0], zm)
-    mail.take(*[("g2", *o) for o in far])
-    g3_buf[g_row] = functools.reduce(jnp.add, [g2_buf[i] for i in range(16)])
-    for dy, dl, dc in others:
-        mail.send(("g3", dy, dl, dc), g3_buf.at[g_row], g3_buf.at[g_row], dev(dy=dy, dl=dl, dc=dc))
-    total = xtotal(1, 0)
-    mail.take(("zr", 1))
-    zs_buf[0] = (total + zr_buf[0].astype(F32)).astype(BF16)
-    mail.send(("z", 0, 1), zs_buf.at[0], z_buf.at[0, 0], zp)
-    total = xtotal(-1, 1)
-    mail.take(("zr", -1))
-    zs_buf[1] = (total + zr_buf[1].astype(F32)).astype(BF16)
-    mail.send(("z", 1, -1), zs_buf.at[1], z_buf.at[1, 1], zm)
-
+    mail.drain("g1")
+    g2_buf[g_col] = functools.reduce(jnp.add, [g1_buf[i] for i in range(16)])
+    far = [(dx, dz) for dx in range(4) for dz in range(4)][1:]
+    piece = g2_buf.at[g_col]
+    mail.burst("g2", g2_buf, [(piece, piece, dev(dx=dx, dz=dz)) for dx, dz in far])
+    mail.settle("al", "ax", "axr", "axf", "az", "azr", "ay", "ak")
+    for dy, peer in ((2, y2), (1, yp), (-1, ym)):
+        ktake(dy, 1)
+        yscatter(1, dy, peer)
+    for d, peer in ((1, zp), (-1, zm)):
+        h = 1 if d == 1 else 0
+        s_buf[d % 4, h] = xtotal(d, h).astype(BF16)
+        zsend_half(d, h, peer)
+    for dy, peer in ((2, y2), (1, yp), (-1, ym)):
+        ktake(dy, 0)
+        yscatter(0, dy, peer)
+    ktake(0, 1)
+    ktake(0, 0)
+    for d, peer in ((1, zp), (-1, zm)):
+        h = 0 if d == 1 else 1
+        total = xtotal(d, h)
+        mail.take(("zr", d))
+        s_buf[d % 4, h] = (total + zr_buf[h].astype(F32)).astype(BF16)
+        zsend_half(d, h, peer)
+    mail.settle("xr", "xf", "x", "zr", "k")
     u_buf[...] = ytotal(1).astype(BF16)
     mail.send(("l",), u_buf, l_buf, lo)
+    mail.drain("g2")
+    g3_buf[g_row] = functools.reduce(jnp.add, [g2_buf[i] for i in range(16)])
+    piece = g3_buf.at[g_row]
+    mail.burst("g3", g3_buf, [(piece, piece, dev(dy=dy, dl=dl, dc=dc)) for dy, dl, dc in others])
+
+    mail.settle("y")
     mine = ytotal(0)
+    mail.take(*[("z", d, h) for d in (1, -1) for h in (0, 1)])
     for h in range(2):
         total = xtotal(0, h)
-        mail.take(("z", h, 1), ("z", h, -1))
-        agg_ref[h] = (total + z_buf[0, h].astype(F32) + z_buf[1, h].astype(F32)).astype(BF16)
-    mail.take(*[("g3", *o) for o in others])
+        for i in range(2):
+            total = total + z_buf[i, h].astype(F32)
+        agg_ref[h] = total.astype(BF16)
+    mail.drain("g3")
     for i in range(16):
         wg_ref[8 * i : 8 * i + 8] = g3_buf[i]
     mail.take(("l",))
@@ -424,7 +475,7 @@
     mail.finish()
 
 
-FIRST = 11 * UNROLL
+STOPS = (0, 6 * UNROLL, 12 * UNROLL, 17 * UNROLL, PAIRS)
 
 
 def layer(features, cotangent, weight, rows, cols, live, values):
@@ -441,11 +492,12 @@
             pltpu.VMEM(b, BF16), pltpu.VMEM((1, SLOTS), I32), pltpu.VMEM((1, SLOTS), I32),
             blocks(BLOCKS), blocks(BLOCKS), blocks(SLOTS + 1), blocks(PAIRS + 1), blocks(BLOCKS),
             blocks(BLOCKS), blocks(8, 2, 2), piece,
-            pltpu.VMEM((8, LISTED), I32), pltpu.VMEM((8, LISTED), I32), pltpu.SMEM((8, LISTED), I32),
-            blocks(4, 2), blocks(4, 2, 2), blocks(4, 2), blocks(2), blocks(2, 2), blocks(2), blocks(4, 2),
+            pltpu.VMEM((8, LISTED), I32), pltpu.VMEM((8, LISTED), I32), pltpu.VMEM((8, LISTED), I32),
+            pltpu.SMEM((8, LISTED), I32), pltpu.SMEM((8, LISTED), I32),
+            blocks(4, 2), blocks(4, 2, 2), blocks(4, 2), blocks(3, 2), blocks(2), blocks(2, 2), blocks(4, 2),
             blocks(8, 2), blocks(8, 2), blocks(2, 3, 2), blocks(2), blocks(2),
             piece, piece, piece,
-            pltpu.SemaphoreType.DMA((5,)), pltpu.SemaphoreType.DMA((CHUNKS,)), pltpu.SemaphoreType.DMA(()),
+            pltpu.SemaphoreType.DMA((5,)), pltpu.SemaphoreType.DMA((CHUNKS,)), pltpu.SemaphoreType.DMA((2,)),
             pltpu.SemaphoreType.DMA((COPIES,)), pltpu.SemaphoreType.DMA((COPIES,)),
         ],
         compiler_params=pltpu.CompilerParams(

time: 55.9 us -> 55.1 us (0.986)
  Pallas kernels: 54.5 us -> 53.6 us
    pallas_call x1, Pallas kernels: 52.8 us -> 51.9 us  [layer(): pl.pallas_call(layer_kernel, out_shape=(own, jax.ShapeDtypeStruct(b, F32)...]
where the time goes in v4:
time: 55.1 us; the launch traced here: 54.9 us
  Pallas kernels  53.6 us (97%)
  between operations  1.29 us (2%)
    pallas_call x1, Pallas kernels, layer(): pl.pallas_call(layer_kernel, out_shape=(own, jax.ShapeDtypeStruct(b, F32)...  51.9 us
    pallas_call x1, Pallas kernels, finish(): pl.pallas_call(functools.partial(finish_kernel, scale), out_shape=shapes,...  1.71 us

profile of v4, /device:TPU:1, one launch (start us, length us, event | category | flops | bytes accessed | tf_op | source)
XLA Modules:
  0.0 54.9 jit_solution(13816188223886809504)
XLA Ops:
  1.3 51.9 %layer.1 = (bf16[2,128,128]{2,1,0:T(8,128)(2,1)}, f32[128,128]{1,0:T(8,128)}, bf16[2,128,128]{2,1,0:T(8,128)(2,1)}) custom-call(bf16[2,128,128]{2,1,0:T(8,128)(2,1)} %bitcast.10, bf16[2,128,128]{2,1,0:T(8,128)(2,1)} %bitcast.11, bf16[128,128]{1,0:T(8,128)(2,1)} %w_ref.1, s32[1,320]{1,0:T(1,128)} %bitcast.14, s32[1,320]{1,0:T(1,128)} %bitcast.15, ...), custom_call_target="tpu_custom_call" | custom-call | tf_op jit(solution)/shard_map/layer/pallas_call | solution.py:486
  53.2 1.7 %finish.1 = (bf16[256,128]{1,0:T(8,128)(2,1)}, f32[128,128]{1,0:T(8,128)}, bf16[256,128]{1,0:T(8,128)(2,1)}) custom-call(bf16[256,128]{1,0:T(8,128)(2,1)} %bitcast.12, bf16[128,128]{1,0:T(8,128)(2,1)} %w_ref.1, f32[128,128]{1,0:T(8,128)} %get-tuple-element.10.g_ref, bf16[256,128]{1,0:T(8,128)(2,1)} %bitcast.13), custom_call_target="tpu_custom_call" | custom-call | tf_op jit(solution)/shard_map/finish/pallas_call | solution.py:518
